TPU v7x, 256 devices: a whole 4x4x8 slice. The times are simulated.
256 devices in a mesh: dp: 32 (over y, x, core), tensor: 8 (over z).
Axes of the slice: x: 4, y: 4, z: 8, core: 2. Of those that a mesh axis runs over, the one named last changes fastest.
Arguments:
- hidden: bfloat16 [16384, 4096], P('dp', 'tensor')
- w_query: bfloat16 [4096, 4096], P(None, 'tensor')
- w_key: bfloat16 [4096, 1024], P(None, 'tensor')
- w_value: bfloat16 [4096, 1024], P(None, 'tensor'), may hold values from -0.09375 to 0.09375
- w_out: bfloat16 [4096, 4096], P('tensor'), may hold values from -0.09375 to 0.09375
- doc_ids: int32 [16384], P('dp'), may hold values from 0 to 16383, as said below
- send_counts: int32 [32, 32], replicated, may hold values from 0 to 16, as said below
Outputs:
- attended: bfloat16 [32768, 4096], P('dp', 'tensor')
Inputs may be any that keep to these rules, and one draw needn't show every extreme that they name: `send_counts`: the diagonal is zero and each row sums to less than 512. On index i of dp the rows that stay come first, then the rows for each destination j in increasing order of j, each such block one whole document. `doc_ids`: the rows of one document lie together on one index of dp and share one id; different documents have different ids.
All inputs are finite; a program needn't handle non-finite values.
Results may differ from a plain program's by a relative error of at most 0.014.
Values may be sent and summed in bfloat16 or wider, within the bound.
No kernel may reach another device: no remote copies, remote signals or barrier semaphores. Data moves between devices by JAX's collectives and lax.ppermute only.
A program may use at most 128 MiB of HBM per device.

v0:
```python
import jax
import jax.numpy as jnp
from jax import lax
from jax.sharding import PartitionSpec as P

HD = 128
SLOT = 16


def project_three(inputs, w_query, w_key, w_value):
    return tuple(
        (
            jnp.dot(inputs, weight, preferred_element_type=jnp.float32).astype(jnp.bfloat16)
            for weight in (w_query, w_key, w_value)
        )
    )


def project_slots(arrived, w_query, w_key, w_value):
    peers, slot_count = (arrived.shape[0], arrived.shape[1])
    flat = arrived.reshape(peers * slot_count, arrived.shape[2])
    return tuple(
        (
            result.reshape(peers, slot_count, -1)
            for result in project_three(flat, w_query, w_key, w_value)
        )
    )


def attend(queries, key_rows, value_rows, allowed, head_dim):
    batch, count = (queries.shape[0], queries.shape[1])
    kv_heads = key_rows.shape[2] // head_dim
    group = queries.shape[2] // key_rows.shape[2]
    query_part = queries.reshape(batch, count, kv_heads, group, head_dim)
    key_part = key_rows.reshape(batch, key_rows.shape[1], kv_heads, head_dim)
    value_part = value_rows.reshape(batch, value_rows.shape[1], kv_heads, head_dim)
    scores = jnp.einsum(
        "bqhgd,bkhd->bhgqk", query_part, key_part, preferred_element_type=jnp.float32
    ) * head_dim ** (-0.5)
    scores = jnp.where(allowed[:, None, None], scores, -jnp.inf)
    top = jnp.max(scores, axis=-1, keepdims=True)
    expo = jnp.exp(scores - top)
    total = jnp.sum(expo, axis=-1)
    mixed = jnp.einsum(
        "bhgqk,bkhd->bqhgd",
        expo.astype(jnp.bfloat16),
        value_part,
        preferred_element_type=jnp.float32,
    )
    mixed = mixed / jnp.transpose(total, (0, 3, 1, 2))[..., None]
    return mixed.reshape(batch, count, -1).astype(jnp.bfloat16)


def on_device(hidden, w_query, w_key, w_value, w_out, doc_ids, send_counts):
    peers = lax.axis_size("dp")
    my_index = lax.axis_index("dp")
    row_count = hidden.shape[0]
    head_dim = HD
    slot_count = SLOT
    home_full = lax.all_gather(hidden, "tensor", axis=1, tiled=True)
    home_q, home_k, home_v = project_three(home_full, w_query, w_key, w_value)
    outgoing = lax.dynamic_slice_in_dim(send_counts, my_index, 1, 0)[0]
    incoming = lax.dynamic_slice_in_dim(send_counts, my_index, 1, 1)[:, 0]
    home_len = row_count - jnp.sum(outgoing)
    block_start = home_len + jnp.cumsum(outgoing) - outgoing
    slot_ids = jnp.arange(slot_count, dtype=jnp.int32)
    peer_ids = jnp.arange(peers, dtype=jnp.int32)
    send_index = jnp.minimum(block_start[:, None] + slot_ids[None, :], row_count - 1).reshape(-1)
    send_valid = slot_ids[None, :] < outgoing[:, None]
    taken = jnp.take(home_full, send_index, axis=0).reshape(peers, slot_count, home_full.shape[1])
    moved = lax.all_to_all(
        jnp.where(send_valid[:, :, None], taken, jnp.zeros((), home_full.dtype)),
        "dp",
        split_axis=0,
        concat_axis=0,
        tiled=True,
    )
    recv_q, recv_k, recv_v = project_slots(moved, w_query, w_key, w_value)
    recv_valid = slot_ids[None, :] < incoming[:, None]
    home_pos = jnp.arange(row_count, dtype=jnp.int32)
    recv_labels = jnp.where(
        recv_valid,
        -1 - peer_ids[:, None],
        -1 - peers - peer_ids[:, None] * slot_count - slot_ids[None, :],
    )
    labels = jnp.concatenate([doc_ids, recv_labels.reshape(-1)])
    all_q = jnp.concatenate([home_q, recv_q.reshape(peers * slot_count, -1)], axis=0)
    all_k = jnp.concatenate([home_k, recv_k.reshape(peers * slot_count, -1)], axis=0)
    all_v = jnp.concatenate([home_v, recv_v.reshape(peers * slot_count, -1)], axis=0)
    positions = jnp.arange(labels.shape[0], dtype=jnp.int32)
    allowed = (labels[:, None] == labels[None, :]) & (positions[None, :] <= positions[:, None])
    mixed = attend(all_q[None], all_k[None], all_v[None], allowed[None], head_dim)[0]
    valid = jnp.concatenate([home_pos < home_len, recv_valid.reshape(-1)])
    partial_sum = jnp.dot(mixed, w_out, preferred_element_type=jnp.float32)
    partial_sum = jnp.where(valid[:, None], partial_sum, 0.0)
    return lax.psum_scatter(
        partial_sum.astype(jnp.bfloat16), "tensor", scatter_dimension=1, tiled=True
    )


def solution(mesh):
    in_specs = (
        P("dp", "tensor"),
        P(None, "tensor"),
        P(None, "tensor"),
        P(None, "tensor"),
        P("tensor", None),
        P("dp"),
        P(),
    )
    out_specs = P("dp", "tensor")
    return jax.shard_map(
        on_device, mesh=mesh, in_specs=in_specs, out_specs=out_specs, check_vma=False
    )
```

profile of v0, /device:TPU:1, one launch (start us, length us, event | category | flops | bytes accessed | tf_op | source)
XLA Modules:
  0.0 273.2 jit_solution(15379162874584786836)
XLA Ops:
  6.5 0.7 all-gather.2.cloned.1.call-update
  7.3 1.3 fusion.22
  8.6 0.1 copy.11
  9.4 0.1 add_reduce_fusion
  9.5 0.1 add_minimum_fusion
  9.6 0.1 min.22
  9.7 0.1 iota_compare_fusion.1
  9.8 57.8 %all-gather.2.cloned.1.call-done = bf16[512,4096]{1,0:T(8,128)(2,1)} async-done(((bf16[512,512]{1,0:T(8,128)(2,1)}), bf16[512,4096]{1,0:T(8,128)(2,1)}) %all-gather.2.cloned.1.call-update) | async-done | bytes 4194320 | tf_op jit(solution)/shard_map/all_gather | solution.py:60
  67.5 11.3 %gather_fusion = bf16[512,4096]{1,0:T(8,128)(2,1)} fusion(bf16[512,4096]{1,0:T(8,128)(2,1)} %all-gather.2.cloned.1.call-done, s32[1024]{0:T(1024)S(1)} %pad_clamp_fusion), kind=kCustom, calls=%fused_computation | custom fusion | bytes 8390656 | tf_op jit(solution)/shard_map/jit(_take)/gather | solution.py:70
  78.8 3.9 %select_select_fusion = bf16[32,16,4096]{2,1,0:T(8,128)(2,1)} fusion(bf16[32,16,4096]{2,1,0:T(8,128)(2,1)} %bitcast.69, pred[32,16]{1,0:T(8,128)(4,1)S(1)} %get-tuple-element.10, pred[32,16]{1,0:T(8,128)(4,1)S(1)} %get-tuple-element.9), kind=kLoop, calls=%fused_computation.11 | loop fusion | flops 4194304 | bytes 8389632 | tf_op jit(solution)/shard_map/jit(_where)/select_n | solution.py:72
  82.7 7.9 %all-to-all-start = ((bf16[32,16,4096]{2,1,0:T(8,128)(2,1)}), bf16[32,16,4096]{2,1,0:T(8,128)(2,1)}, u32[]{:S(2)}, u32[]{:S(2)}) async-start(bf16[32,16,4096]{2,1,0:T(8,128)(2,1)} %select_select_fusion), calls=%async_computation | async-start | bytes 8388608 | tf_op jit(solution)/shard_map/all_to_all | solution.py:71
  90.6 0.2 reduce-scatter.2.cloned.1.call-start
  90.9 0.2 dynamic-slice_reduce_fusion
  91.1 0.1 iota_compare_fusion.2
  91.1 0.1 lt.82
  91.3 0.1 sub.63
  91.4 0.1 broadcast_in_dim.76
  91.5 0.1 broadcast_in_dim.77
  91.6 0.6 fusion.7
  92.3 4.0 %convolution_convert_fusion.5 = bf16[512,128]{0,1:T(8,128)(2,1)S(1)} fusion(bf16[512,4096]{1,0:T(8,128)(2,1)} %all-gather.2.cloned.1.call-done, bf16[4096,128]{1,0:T(8,128)(2,1)S(1)} %copy-done.2), kind=kOutput, calls=%fused_computation.20 | convolution fusion | flops 536936448 | bytes 5373952 | tf_op jit(solution)/shard_map/dot_general | solution.py:13
  96.3 1.2 convolution_convert_fusion.3
  97.5 0.9 copy-done.5
  98.5 3.1 %convolution_convert_fusion.1 = bf16[512,512]{1,0:T(8,128)(2,1)} fusion(bf16[512,4096]{1,0:T(8,128)(2,1)S(1)} %copy-done.1, bf16[4096,512]{1,0:T(8,128)(2,1)S(1)} %copy-done.5), kind=kOutput, calls=%fused_computation.16 | convolution fusion | flops 2147745792 | bytes 8912896 | tf_op jit(solution)/shard_map/dot_general | solution.py:13
  101.6 39.7 %all-to-all-done = bf16[32,16,4096]{2,1,0:T(8,128)(2,1)} async-done(((bf16[32,16,4096]{2,1,0:T(8,128)(2,1)}), bf16[32,16,4096]{2,1,0:T(8,128)(2,1)}, u32[]{:S(2)}, u32[]{:S(2)}) %all-to-all-start) | async-done | bytes 4194336 | tf_op jit(solution)/shard_map/all_to_all | solution.py:71
  141.3 3.4 %convolution_convert_fusion.2 = bf16[512,128]{1,0:T(8,128)(2,1)S(1)} fusion(bf16[512,4096]{1,0:T(8,128)(2,1)} %bitcast.4, bf16[4096,128]{1,0:T(8,128)(2,1)S(1)} %copy-done), kind=kOutput, calls=%fused_computation.17 | convolution fusion | flops 536936448 | bytes 5373952 | tf_op jit(solution)/shard_map/dot_general | solution.py:13
  144.8 3.8 %convolution_convert_fusion.4 = bf16[512,128]{0,1:T(8,128)(2,1)S(1)} fusion(bf16[512,4096]{1,0:T(8,128)(2,1)} %bitcast.4, bf16[4096,128]{1,0:T(8,128)(2,1)S(1)} %copy-done.2), kind=kOutput, calls=%fused_computation.19 | convolution fusion | flops 536936448 | bytes 5373952 | tf_op jit(solution)/shard_map/dot_general | solution.py:13
  148.6 4.6 %convolution_convert_fusion = bf16[512,512]{1,0:T(8,128)(2,1)S(1)} fusion(bf16[512,4096]{1,0:T(8,128)(2,1)} %bitcast.4, bf16[4096,512]{1,0:T(8,128)(2,1)S(1)} %copy-done.6), kind=kOutput, calls=%fused_computation.15 | convolution fusion | flops 2147745792 | bytes 8912896 | tf_op jit(solution)/shard_map/dot_general | solution.py:13
  153.2 3.1 %fusion.2 = (f32[4,1024]{1,0:T(4,128)S(1)}, f32[1024,1024,4]{1,0,2:T(8,128)S(1)}) fusion(pred[1024,1024]{0,1:T(8,128)(4,1)S(1)} %fusion.7, bf16[512,128]{1,0:T(8,128)(2,1)S(1)} %convolution_convert_fusion.2, bf16[512,128]{1,0:T(8,128)(2,1)S(1)} %convolution_convert_fusion.3, bf16[512,512]{1,0:T(8,128)(2,1)S(1)} %convolution_convert_fusion, ...), kind=kOutput, calls=%fused_computation.6 | convolution fusion | flops 1088942080 | bytes 19152896 | tf_op jit(solution)/shard_map/bqhgd,bkhd->bhgqk/dot_general | solution.py:37
  156.3 3.9 %fusion = f32[4,1024]{1,0:T(4,128)S(1)} fusion(f32[1024,1024,4]{1,0,2:T(8,128)S(1)} %get-tuple-element.8, f32[4,1024]{1,0:T(4,128)S(1)} %get-tuple-element.7, pred[1024,1024]{0,1:T(8,128)(4,1)S(1)} %fusion.7), kind=kLoop, calls=%fused_computation.4 | loop fusion | flops 16773120 | bytes 17858560 | tf_op jit(solution)/shard_map/reduce_sum | solution.py:43
  160.2 5.2 %fusion.8 = bf16[1,1024,1,4,128]{1,4,3,2,0:T(8,128)(2,1)S(1)} fusion(f32[1024,1024,4]{1,0,2:T(8,128)S(1)} %get-tuple-element.8, f32[4,1024]{1,0:T(4,128)S(1)} %get-tuple-element.7, pred[1024,1024]{0,1:T(8,128)(4,1)S(1)} %fusion.7, f32[1024,4]{0,1:T(4,128)S(1)} %bitcast.70, bf16[512,128]{0,1:T(8,128)(2,1)S(1)} %convolution_convert_fusion.4, ...), kind=kOutput, calls=%fused_computation.14 | convolution fusion | flops 1092091904 | bytes 19169280 | tf_op jit(solution)/shard_map/bhgqk,bkhd->bqhgd/dot_general | solution.py:44
  165.3 9.0 %select_convert_fusion = bf16[1024,4096]{1,0:T(8,128)(2,1)} fusion(pred[1024]{0:T(1024)(128)(4,1)S(1)} %pad_add_fusion.1, bf16[1024,512]{0,1:T(8,128)(2,1)S(1)} %bitcast.74, bf16[512,4096]{1,0:T(8,128)(2,1)} %param.11), kind=kOutput, calls=%fused_computation.2 | convolution fusion | flops 4303355904 | bytes 13632512 | tf_op jit(solution)/shard_map/dot_general | solution.py:94
  174.4 91.9 %reduce-scatter.2.cloned.1.call-done = bf16[1024,512]{1,0:T(8,128)(2,1)} async-done(((bf16[1024,4096]{1,0:T(8,128)(2,1)}), bf16[1024,512]{1,0:T(8,128)(2,1)}) %reduce-scatter.2.cloned.1.call-update) | async-done | bytes 1048592 | tf_op jit(solution)/shard_map/reduce_scatter | solution.py:96
  (28 shorter events, 0.2 us)
Async XLA Ops:
  6.5 89.7 %copy-start = (bf16[4096,128]{1,0:T(8,128)(2,1)S(1)}, bf16[4096,128]{1,0:T(8,128)(2,1)}, u32[]{:S(2)}) copy-start(bf16[4096,128]{1,0:T(8,128)(2,1)} %param.9) | copy-start | bytes 3145732
  6.5 61.0 %all-gather.2.cloned.1.call-start = ((), (), s32[]{:S(2)}) async-start(), calls=%async_computation.2 | async-start | bytes 4718592 | tf_op jit(solution)/shard_map/all_gather | solution.py:60
  82.7 8.1 %copy-start.3 = (s32[32,32]{1,0:T(8,128)S(1)}, s32[32,32]{1,0:T(8,128)}, u32[]{:S(2)}) copy-start(s32[32,32]{1,0:T(8,128)} %param.13) | copy-start | bytes 12292
  82.7 8.9 %copy-start.4 = (s32[512]{0:T(512)S(1)}, s32[512]{0:T(512)}, u32[]{:S(2)}) copy-start(s32[512]{0:T(512)} %param.12) | copy-start | bytes 6148
  82.7 9.5 %copy-start.2 = (bf16[4096,128]{1,0:T(8,128)(2,1)S(1)}, bf16[4096,128]{1,0:T(8,128)(2,1)}, u32[]{:S(2)}) copy-start(bf16[4096,128]{1,0:T(8,128)(2,1)} %param.10) | copy-start | bytes 3145732
  82.7 58.6 %all-to-all-start = ((bf16[32,16,4096]{2,1,0:T(8,128)(2,1)}), bf16[32,16,4096]{2,1,0:T(8,128)(2,1)}, u32[]{:S(2)}, u32[]{:S(2)}) async-start(bf16[32,16,4096]{2,1,0:T(8,128)(2,1)} %select_select_fusion), calls=%async_computation | async-start | bytes 8388608 | tf_op jit(solution)/shard_map/all_to_all | solution.py:71
  90.6 175.7 %reduce-scatter.2.cloned.1.call-start = ((), (), s32[]{:S(2)}) async-start(), calls=%async_computation.3 | async-start | bytes 9437184 | tf_op jit(solution)/shard_map/reduce_scatter | solution.py:96
  91.6 4.6 %copy-start.1 = (bf16[512,4096]{1,0:T(8,128)(2,1)S(1)}, bf16[512,4096]{1,0:T(8,128)(2,1)}, u32[]{:S(2)}) copy-start(bf16[512,4096]{1,0:T(8,128)(2,1)} %all-gather.2.cloned.1.call-done) | copy-start | bytes 12582916
  96.3 2.2 copy-start.5
  144.8 3.9 %copy-start.6 = (bf16[4096,512]{1,0:T(8,128)(2,1)S(1)}, bf16[4096,512]{1,0:T(8,128)(2,1)}, u32[]{:S(2)}) copy-start(bf16[4096,512]{1,0:T(8,128)(2,1)} %param.8) | copy-start | bytes 12582916
  148.6 4.6 %copy-start.7 = (bf16[512,512]{1,0:T(8,128)(2,1)S(1)}, bf16[512,512]{1,0:T(8,128)(2,1)}, u32[]{:S(2)}) copy-start(bf16[512,512]{1,0:T(8,128)(2,1)} %convolution_convert_fusion.1) | copy-start | bytes 1572868
Sparse Core Ops, SparseCore 0:
  9.1 58.3 all-gather.1
  174.5 91.7 reduce-scatter.1
where the time goes:
time: 273 us
  waiting for transfers between devices  190 us (70%)
  matrix products  37.5 us (14%)
  between operations  14.3 us (5%)
  local copies, waits for them, and re-layouts  12.9 us (5%)
  other arithmetic  10.2 us (4%)
  starting transfers between devices  8.11 us (3%)
    reduce_scatter x1, waiting for transfers between devices, on_device(): lax.psum_scatter(partial_sum.astype(jnp.bfloat16), 'tensor', scatter_dime...  91.9 us
    all_gather x1, waiting for transfers between devices, on_device(): home_full = lax.all_gather(hidden, 'tensor', axis=1, tiled=True)  57.8 us
    all_to_all x1, waiting for transfers between devices, on_device(): lax.all_to_all(jnp.where(send_valid[:, :, None], taken, jnp.zeros((), hom...  39.7 us
    dot_general x6, matrix products, project_three(): jnp.dot(inputs, weight, preferred_element_type=jnp.float32)  20.2 us
    gather x1, local copies, waits for them, and re-layouts, on_device(): jnp.take(home_full, send_index, axis=0)  11.3 us
    dot_general x1, matrix products, on_device(): partial_sum = jnp.dot(mixed, w_out, preferred_element_type=jnp.float32)  9.03 us
    all_to_all x1, starting transfers between devices, on_device(): lax.all_to_all(jnp.where(send_valid[:, :, None], taken, jnp.zeros((), hom...  7.89 us
  transfers between devices with their start and end apart: 3, of which 3 were waited for; matrix products, arithmetic and copies ran while one was open for 4% of the time, Pallas kernels for 0%

commit v1 on v0

v1 whole, which is shorter than its diff:
```python
import jax
import jax.numpy as jnp
from jax import lax
from jax.sharding import PartitionSpec as P

HD = 128
SLOT = 16


def attend(queries, keys, values, allowed):
    count = queries.shape[0]
    kv_heads = keys.shape[1] // HD
    group = queries.shape[1] // keys.shape[1]
    query_part = queries.reshape(count, kv_heads, group, HD)
    key_part = keys.reshape(count, kv_heads, HD)
    value_part = values.reshape(count, kv_heads, HD)
    scores = jnp.einsum(
        "qhgd,khd->hgqk", query_part, key_part, preferred_element_type=jnp.float32
    ) * HD ** (-0.5)
    scores = jnp.where(allowed[None, None], scores, -jnp.inf)
    top = jnp.max(scores, axis=-1, keepdims=True)
    expo = jnp.exp(scores - top)
    total = jnp.sum(expo, axis=-1)
    mixed = jnp.einsum(
        "hgqk,khd->qhgd",
        expo.astype(jnp.bfloat16),
        value_part,
        preferred_element_type=jnp.float32,
    )
    mixed = mixed / jnp.transpose(total, (2, 0, 1))[..., None]
    return mixed.reshape(count, -1).astype(jnp.bfloat16)


def on_device(hidden, w_query, w_key, w_value, w_out, doc_ids, send_counts):
    peers = lax.axis_size("dp")
    me = lax.axis_index("dp")
    rows = hidden.shape[0]
    pos = jnp.arange(rows, dtype=jnp.int32)

    outgoing = lax.dynamic_slice_in_dim(send_counts, me, 1, 0)[0]
    home_len = rows - jnp.sum(outgoing)
    block_start = home_len + jnp.cumsum(outgoing) - outgoing
    slot_ids = jnp.arange(SLOT, dtype=jnp.int32)
    send_row = block_start[:, None] + slot_ids[None, :]
    send_row = jnp.where(slot_ids[None, :] < outgoing[:, None], send_row, -1)
    pick = (send_row.reshape(-1)[:, None] == pos[None, :]).astype(jnp.bfloat16)

    full = lax.all_gather(hidden, "tensor", axis=1, tiled=True)
    query, key, value = (
        jnp.dot(full, weight, preferred_element_type=jnp.float32).astype(jnp.bfloat16)
        for weight in (w_query, w_key, w_value)
    )
    allowed = (doc_ids[:, None] == doc_ids[None, :]) & (pos[None, :] <= pos[:, None])
    mixed = attend(query, key, value, allowed)
    partial_sum = jnp.dot(mixed, w_out, preferred_element_type=jnp.float32).astype(jnp.bfloat16)
    done = lax.psum_scatter(partial_sum, "tensor", scatter_dimension=1, tiled=True)

    home = jnp.where((pos < home_len)[:, None], done, jnp.zeros((), done.dtype))
    leaving = jnp.dot(pick, done, preferred_element_type=jnp.float32).astype(done.dtype)
    leaving = leaving.reshape(peers, SLOT, -1)
    arrived = lax.all_to_all(leaving, "dp", split_axis=0, concat_axis=0, tiled=True)
    return jnp.concatenate([home, arrived.reshape(peers * SLOT, -1)], axis=0)


def solution(mesh):
    in_specs = (
        P("dp", "tensor"),
        P(None, "tensor"),
        P(None, "tensor"),
        P(None, "tensor"),
        P("tensor", None),
        P("dp"),
        P(),
    )
    return jax.shard_map(
        on_device, mesh=mesh, in_specs=in_specs, out_specs=P("dp", "tensor"), check_vma=False
    )
```

time: 273 us -> 180 us (0.66)
  waiting for transfers between devices: 190 us -> 122 us
  local copies, waits for them, and re-layouts: 12.9 us -> 0.18 us
  matrix products: 37.5 us -> 27.8 us
    reduce_scatter x1, waiting for transfers between devices: 91.9 us -> 51.8 us  [on_device(): lax.psum_scatter(partial_sum, 'tensor', scatter_dimension=1, tiled=True)]
    all_to_all x1, waiting for transfers between devices: 39.7 us -> 10.2 us  [on_device(): lax.all_to_all(leaving, 'dp', split_axis=0, concat_axis=0, tiled=True)]
    gather x1 -> x0, local copies, waits for them, and re-layouts: 11.3 us -> none  [on_device(): jnp.take(home_full, send_index, axis=0)]
    dot_general x9 -> x5, matrix products: 37.5 us -> 27.8 us  [the longest x1 7.01 us: attend(): jnp.einsum('qhgd,khd->hgqk', query_part, key_part, preferred_element_type...]
  transfers between devices with their start and end apart: 3 -> 3, of which waited for: 3 -> 3; matrix products, arithmetic and copies ran while one was open for 4% -> 2% of each run, Pallas kernels for 0% -> 0%
where the time goes in v1:
time: 180 us
  waiting for transfers between devices  122 us (68%)
  matrix products  27.8 us (15%)
  between operations  14.1 us (8%)
  other arithmetic  7.94 us (4%)
  starting transfers between devices  7.65 us (4%)
    all_gather x1, waiting for transfers between devices, on_device(): full = lax.all_gather(hidden, 'tensor', axis=1, tiled=True)  59.3 us
    reduce_scatter x1, waiting for transfers between devices, on_device(): lax.psum_scatter(partial_sum, 'tensor', scatter_dimension=1, tiled=True)  51.8 us
    all_to_all x1, waiting for transfers between devices, on_device(): lax.all_to_all(leaving, 'dp', split_axis=0, concat_axis=0, tiled=True)  10.2 us
    all_to_all x1, starting transfers between devices, on_device(): lax.all_to_all(leaving, 'dp', split_axis=0, concat_axis=0, tiled=True)  7.61 us
    dot_general x1, matrix products, attend(): jnp.einsum('qhgd,khd->hgqk', query_part, key_part, preferred_element_type...  7.01 us
    dot_general x1, matrix products, on_device(): jnp.dot(mixed, w_out, preferred_element_type=jnp.float32)  6.49 us
    dot_general x1, matrix products, attend(): jnp.einsum('hgqk,khd->qhgd', expo.astype(jnp.bfloat16), value_part, prefe...  6.11 us
    dot_general x1, matrix products, on_device(): jnp.dot(full, weight, preferred_element_type=jnp.float32)  5.83 us
  transfers between devices with their start and end apart: 3, of which 3 were waited for; matrix products, arithmetic and copies ran while one was open for 2% of the time, Pallas kernels for 0%

profile of v1, /device:TPU:1, one launch (start us, length us, event | category | flops | bytes accessed | tf_op | source)
XLA Modules:
  0.0 179.6 jit_solution(5572601823768428218)
XLA Ops:
  6.5 0.0 copy-start
  6.5 0.0 all-gather.2.cloned.1.call-start
  6.5 0.7 all-gather.2.cloned.1.call-update
  7.3 0.0 reduce-scatter.2.cloned.1.call-start
  7.3 1.0 fusion.13
  8.3 59.3 %all-gather.2.cloned.1.call-done = bf16[512,4096]{1,0:T(8,128)(2,1)} async-done(((bf16[512,512]{1,0:T(8,128)(2,1)}), bf16[512,4096]{1,0:T(8,128)(2,1)}) %all-gather.2.cloned.1.call-update) | async-done | bytes 4194320 | tf_op jit(solution)/shard_map/all_gather | solution.py:48
  67.5 5.8 %convolution_convert_fusion.2 = bf16[512,512]{0,1:T(8,128)(2,1)S(1)} fusion(bf16[512,4096]{1,0:T(8,128)(2,1)} %all-gather.2.cloned.1.call-done, bf16[4096,512]{1,0:T(8,128)(2,1)} %param.8), kind=kOutput, calls=%fused_computation.11 | convolution fusion | flops 2147745792 | bytes 8912896 | tf_op jit(solution)/shard_map/dot_general | solution.py:50
  73.4 0.0 copy-done
  73.4 7.0 %fusion.2 = (f32[4,512]{1,0:T(4,128)S(1)}, f32[512,512,4]{1,0,2:T(8,128)}) fusion(pred[512,512]{0,1:T(8,128)(4,1)S(1)} %fusion.13, bf16[512,4,128]{0,2,1:T(8,128)(2,1)S(1)} %bitcast.64, bf16[512,4096]{1,0:T(8,128)(2,1)} %all-gather.2.cloned.1.call-done, bf16[4096,128]{1,0:T(8,128)(2,1)S(1)} %copy-done), kind=kOutput, calls=%fused_computation.5 | convolution fusion | flops 808515584 | bytes 10231808 | tf_op jit(solution)/shard_map/qhgd,khd->hgqk/dot_general | solution.py:17
  80.4 0.0 copy-start.1
  80.4 3.2 %fusion = f32[4,512]{1,0:T(4,128)S(1)} fusion(f32[512,512,4]{1,0,2:T(8,128)} %get-tuple-element.8, f32[4,512]{1,0:T(4,128)S(1)} %get-tuple-element.7, pred[512,512]{0,1:T(8,128)(4,1)S(1)} %fusion.13), kind=kLoop, calls=%fused_computation.3 | loop fusion | flops 4192256 | bytes 4472832 | tf_op jit(solution)/shard_map/reduce_sum | solution.py:23
  83.6 0.0 copy-done.1
  83.6 6.1 %divide_convert_fusion = bf16[512,1,4,128]{0,3,2,1:T(8,128)(2,1)S(1)} fusion(f32[512,512,4]{1,0,2:T(8,128)} %get-tuple-element.8, f32[4,512]{1,0:T(4,128)S(1)} %get-tuple-element.7, pred[512,512]{0,1:T(8,128)(4,1)S(1)} %fusion.13, bf16[512,4096]{1,0:T(8,128)(2,1)} %all-gather.2.cloned.1.call-done, bf16[4096,128]{1,0:T(8,128)(2,1)S(1)} %copy-done.1, ...), kind=kOutput, calls=%fused_computation.19 | convolution fusion | flops 810090496 | bytes 10240000 | tf_op jit(solution)/shard_map/hgqk,khd->qhgd/dot_general | solution.py:24
  89.7 6.5 %convolution_convert_fusion = bf16[512,4096]{1,0:T(8,128)(2,1)} fusion(bf16[512,512]{0,1:T(8,128)(2,1)S(1)} %bitcast.63, bf16[512,4096]{1,0:T(8,128)(2,1)} %param.11), kind=kOutput, calls=%fused_computation | convolution fusion | flops 2149580800 | bytes 8912896 | tf_op jit(solution)/shard_map/dot_general | solution.py:55
  96.2 0.0 reduce-scatter.2.cloned.1.call-update
  96.2 1.3 fusion.19
  97.6 0.1 copy.13
  97.6 0.1 reduce-window.8
  98.3 0.1 add_reduce_fusion
  98.5 0.1 add_select_fusion
  98.5 0.1 select_n.26
  98.6 51.8 %reduce-scatter.2.cloned.1.call-done = bf16[512,512]{1,0:T(8,128)(2,1)} async-done(((bf16[512,4096]{1,0:T(8,128)(2,1)}), bf16[512,512]{1,0:T(8,128)(2,1)}) %reduce-scatter.2.cloned.1.call-update) | async-done | bytes 524304 | tf_op jit(solution)/shard_map/reduce_scatter | solution.py:56
  150.4 2.3 %convolution_convert_fusion.1 = bf16[512,512]{1,0:T(8,128)(2,1)} fusion(bf16[512,512]{1,0:T(8,128)(2,1)} %reduce-scatter.2.cloned.1.call-done, s32[512]{0:T(512)S(1)} %select_n.26), kind=kOutput, calls=%fused_computation.10 | convolution fusion | flops 268959744 | bytes 1050624 | tf_op jit(solution)/shard_map/dot_general | solution.py:59
  152.7 7.6 %all-to-all-start = ((bf16[32,16,512]{2,1,0:T(8,128)(2,1)}), bf16[32,16,512]{2,1,0:T(8,128)(2,1)S(1)}, u32[]{:S(2)}, u32[]{:S(2)}) async-start(bf16[32,16,512]{2,1,0:T(8,128)(2,1)} %bitcast.14), calls=%async_computation.1 | async-start | bytes 1048576 | tf_op jit(solution)/shard_map/all_to_all | solution.py:61
  160.3 1.2 broadcast_select_fusion
  161.5 10.2 %all-to-all-done = bf16[32,16,512]{2,1,0:T(8,128)(2,1)S(1)} async-done(((bf16[32,16,512]{2,1,0:T(8,128)(2,1)}), bf16[32,16,512]{2,1,0:T(8,128)(2,1)S(1)}, u32[]{:S(2)}, u32[]{:S(2)}) %all-to-all-start) | async-done | bytes 524320 | tf_op jit(solution)/shard_map/all_to_all | solution.py:61
  171.8 1.0 pad_maximum_fusion
  (2 shorter events, 0.0 us)
Async XLA Ops:
  6.5 66.8 %copy-start = (bf16[4096,128]{1,0:T(8,128)(2,1)S(1)}, bf16[4096,128]{1,0:T(8,128)(2,1)}, u32[]{:S(2)}) copy-start(bf16[4096,128]{1,0:T(8,128)(2,1)} %param.9) | copy-start | bytes 3145732
  6.5 61.0 %all-gather.2.cloned.1.call-start = ((), (), s32[]{:S(2)}) async-start(), calls=%async_computation.2 | async-start | bytes 4718592 | tf_op jit(solution)/shard_map/all_gather | solution.py:48
  7.3 143.1 %reduce-scatter.2.cloned.1.call-start = ((), (), s32[]{:S(2)}) async-start(), calls=%async_computation.3 | async-start | bytes 4718592 | tf_op jit(solution)/shard_map/reduce_scatter | solution.py:56
  80.4 3.2 %copy-start.1 = (bf16[4096,128]{1,0:T(8,128)(2,1)S(1)}, bf16[4096,128]{1,0:T(8,128)(2,1)}, u32[]{:S(2)}) copy-start(bf16[4096,128]{1,0:T(8,128)(2,1)} %param.10) | copy-start | bytes 3145732
  152.7 19.1 %all-to-all-start = ((bf16[32,16,512]{2,1,0:T(8,128)(2,1)}), bf16[32,16,512]{2,1,0:T(8,128)(2,1)S(1)}, u32[]{:S(2)}, u32[]{:S(2)}) async-start(bf16[32,16,512]{2,1,0:T(8,128)(2,1)} %bitcast.14), calls=%async_computation.1 | async-start | bytes 1048576 | tf_op jit(solution)/shard_map/all_to_all | solution.py:61
Sparse Core Ops, SparseCore 0:
  9.1 58.3 all-gather.1
  96.3 54.0 reduce-scatter.1

commit v2 on v1

v2 whole, which is shorter than its diff:
```python
import functools

import jax
import jax.numpy as jnp
from jax import lax
from jax.experimental import pallas as pl
from jax.experimental.pallas import tpu as pltpu
from jax.sharding import PartitionSpec as P


HD = 128
SLOT = 16
BF = jnp.bfloat16
F32 = jnp.float32
SPLIT = 8
VMEM_LIMIT = 14 * 1024 * 1024


def ring_offsets(n_ring):
    offsets = [0]
    for s in range(1, n_ring // 2):
        offsets += [-s, s]
    return offsets + [n_ring // 2]


def block_start(offset, n_ring, width):
    me = lax.axis_index("tensor")
    return pl.multiple_of(lax.rem(me + (offset + n_ring), n_ring) * width, width)


def project_in(shards, wq, wk, wv, x):
    n_ring = len(shards)
    width = shards[0].shape[1]
    for shard, off in zip(shards, ring_offsets(n_ring)):
        x[:, pl.ds(block_start(off, n_ring, width), width)] = shard[...]
    rows = x[...]
    return tuple(
        jnp.dot(rows, w[...], preferred_element_type=F32).astype(BF) for w in (wq, wk, wv)
    )


def attend(query, key, value, ids, base):
    rows, keys = query.shape[0], key.shape[0]
    row = lax.broadcasted_iota(jnp.int32, (rows, keys), 0) + base
    col = lax.broadcasted_iota(jnp.int32, (rows, keys), 1)
    across = jnp.broadcast_to(ids[...], (HD, ids.shape[1]))
    down = jnp.transpose(across)[base : base + rows, :1]
    allowed = (down == ids[:, :keys]) & (col <= row)
    heads = []
    for h in range(query.shape[1] // HD):
        scores = lax.dot_general(
            query[:, h * HD : (h + 1) * HD],
            key,
            (((1,), (1,)), ((), ())),
            preferred_element_type=F32,
        ) * (HD ** -0.5)
        scores = jnp.where(allowed, scores, -jnp.inf)
        expo = jnp.exp(scores - jnp.max(scores, axis=-1, keepdims=True))
        total = jnp.sum(expo, axis=-1, keepdims=True)
        head = jnp.dot(expo.astype(BF), value, preferred_element_type=F32)
        heads.append((head / total).astype(BF))
    return jnp.concatenate(heads, axis=1)


def project_out(mixed, wo, offsets, n_ring, outs):
    width = wo.shape[1] // n_ring
    for out, off in zip(outs, offsets):
        block = wo[:, pl.ds(block_start(off, n_ring, width), width)]
        out[...] = jnp.dot(mixed, block, preferred_element_type=F32).astype(BF)


def first_kernel(n_ring, offsets, base, *refs):
    shards = refs[:n_ring]
    wq, wk, wv, wo, ids, mixed_out, k_out, v_out, *outs, x = refs[n_ring:]
    query, key, value = project_in(shards, wq, wk, wv, x)
    k_out[...] = key
    v_out[...] = value
    mixed = attend(query, key, value, ids, base)
    mixed_out[...] = mixed
    project_out(mixed, wo, offsets, n_ring, outs)


def qkv_kernel(n_ring, offsets, base, *refs):
    shards = refs[:n_ring]
    wq, wk, wv, q_out, k_out, v_out, x = refs[n_ring:]
    q_out[...], k_out[...], v_out[...] = project_in(shards, wq, wk, wv, x)


def attend_kernel(n_ring, offsets, base, q, k0, v0, k1, v1, wo, ids, mixed_out, *outs):
    key = jnp.concatenate([k0[...], k1[...]], axis=0)
    value = jnp.concatenate([v0[...], v1[...]], axis=0)
    mixed = attend(q[...], key, value, ids, base)
    mixed_out[...] = mixed
    project_out(mixed, wo, offsets, n_ring, outs)


def rest_kernel(n_ring, offsets, base, mixed, wo, *outs):
    project_out(mixed[...], wo, offsets, n_ring, outs)


def plan_kernel(counts, pick):
    peers = counts.shape[1]
    rows = pick.shape[1]
    me = lax.axis_index("dp")
    start = rows - lax.fori_loop(0, peers, lambda j, n: n + counts[me, j], 0)
    slot = lax.broadcasted_iota(jnp.int32, (SLOT, rows), 0)
    gap = lax.broadcasted_iota(jnp.int32, (SLOT, rows), 1) - slot

    def step(j, start):
        count = counts[me, j]
        hit = (gap == start) & (slot < count)
        at = pl.multiple_of(j * SLOT, SLOT)
        pick[pl.ds(at, SLOT), :] = hit.astype(F32).astype(BF)
        return start + count

    lax.fori_loop(0, peers, step, start)


def touch_kernel(*refs):
    refs[-1][...] = jnp.zeros(refs[-1].shape, BF)


def finish_kernel(counts, pick, own_a, up_a, down_a, own_b, up_b, down_b, *refs):
    *_, leaving, home = refs
    total_a = own_a[...].astype(F32) + up_a[...].astype(F32) + down_a[...].astype(F32)
    total_b = own_b[...].astype(F32) + up_b[...].astype(F32) + down_b[...].astype(F32)
    done = jnp.concatenate([total_a, total_b], axis=0)
    leaving[...] = jnp.dot(pick[...], done.astype(BF), preferred_element_type=F32).astype(BF)
    rows = done.shape[0]
    me = lax.axis_index("dp")
    kept = rows - lax.fori_loop(0, counts.shape[1], lambda j, n: n + counts[me, j], 0)
    row = lax.broadcasted_iota(jnp.int32, done.shape, 0)
    home[...] = jnp.where(row < kept, done, 0.0).astype(BF)


def call(kernel, operands, outs, scratch=(), scalars=0):
    vmem = pl.BlockSpec(memory_space=pltpu.VMEM)
    smem = pl.BlockSpec(memory_space=pltpu.SMEM)
    return pl.pallas_call(
        kernel,
        out_shape=[jax.ShapeDtypeStruct(shape, BF) for shape in outs],
        in_specs=[smem] * scalars + [vmem] * (len(operands) - scalars),
        out_specs=[vmem] * len(outs),
        scratch_shapes=scratch,
        compiler_params=pltpu.CompilerParams(vmem_limit_bytes=VMEM_LIMIT),
    )(*operands)


def on_device(hidden, w_query, w_key, w_value, w_out, doc_ids, send_counts):
    peers = lax.axis_size("dp")
    n_ring = lax.axis_size("tensor")
    rows, width = hidden.shape
    kv = w_key.shape[1]
    cut = rows * SPLIT // 16
    up = [(i, (i + 1) % n_ring) for i in range(n_ring)]
    down = [(i, (i - 1) % n_ring) for i in range(n_ring)]

    def send(x, go_up):
        return lax.ppermute(x, "tensor", up if go_up else down)

    def gather(block, far_up):
        shards, a, b = [block], block, block
        for _ in range(n_ring // 2 - 1):
            a, b = send(a, True), send(b, False)
            shards += [a, b]
        return shards + [send(a if far_up else b, far_up)]

    def add(x, y):
        return (x.astype(F32) + y.astype(F32)).astype(BF)

    def reduce(parts, far_up):
        a = send(parts[0], far_up)
        b = None
        for s in range(n_ring // 2 - 1):
            to_up, to_down = parts[1 + 2 * s], parts[2 + 2 * s]
            if s == 0:
                if far_up:
                    a, b = add(to_up, a), to_down
                else:
                    a, b = to_up, add(to_down, a)
            else:
                a, b = add(to_up, a), add(to_down, b)
            a, b = send(a, True), send(b, False)
        return parts[-1], a, b

    w_in = (w_query, w_key, w_value)
    ids = doc_ids[None, :]
    (pick,) = call(plan_kernel, (send_counts,), [(peers * SLOT, rows)], scalars=1)
    (mark_out,) = call(touch_kernel, (w_out, w_query), [(SLOT, HD)])
    (mark_in,) = call(touch_kernel, (w_key, w_value), [(SLOT, HD)])
    shards_a = gather(hidden[:cut], True)
    shards_b = gather(hidden[cut:], False)
    order = ring_offsets(n_ring)[::-1]
    tile_a, tile_b, kv_a, kv_b = (cut, width), (rows - cut, width), (cut, kv), (rows - cut, kv)
    lead_a, lead_b = (order[0], order[2]), (order[0], order[1])
    late_a = tuple(o for o in order if o not in lead_a)
    late_b = tuple(o for o in order if o not in lead_b)

    def body(kernel, offsets=(), base=0):
        return functools.partial(kernel, n_ring, offsets, base)

    mixed_a, key_a, value_a, *first_a = call(
        body(first_kernel, lead_a), (*shards_a, *w_in, w_out, ids),
        [tile_a, kv_a, kv_a, tile_a, tile_a], [pltpu.VMEM((cut, n_ring * width), BF)],
    )
    rest_a = call(body(rest_kernel, late_a), (mixed_a, w_out), [tile_a] * len(late_a))
    query_b, key_b, value_b = call(
        body(qkv_kernel), (*shards_b, *w_in), [tile_b, kv_b, kv_b],
        [pltpu.VMEM((rows - cut, n_ring * width), BF)],
    )
    mixed_b, *first_b = call(
        body(attend_kernel, lead_b, cut),
        (query_b, key_a, value_a, key_b, value_b, w_out, ids), [tile_b] * 3,
    )
    rest_b = call(body(rest_kernel, late_b), (mixed_b, w_out), [tile_b] * len(late_b))
    parts_a = dict(zip(lead_a + late_a, [*first_a, *rest_a]))
    parts_b = dict(zip(lead_b + late_b, [*first_b, *rest_b]))
    sums_a = reduce([parts_a[o] for o in order], True)
    sums_b = reduce([parts_b[o] for o in order], False)
    leaving, home = call(
        finish_kernel, (send_counts, pick, *sums_a, *sums_b, mark_out, mark_in),
        [(peers * SLOT, width), (rows, width)], scalars=1,
    )
    leaving = leaving.reshape(peers, SLOT, width)
    arrived = lax.all_to_all(leaving, "dp", split_axis=0, concat_axis=0, tiled=True)
    return jnp.concatenate([home, arrived.reshape(peers * SLOT, width)], axis=0)


def solution(mesh):
    in_specs = (
        P("dp", "tensor"),
        P(None, "tensor"),
        P(None, "tensor"),
        P(None, "tensor"),
        P("tensor", None),
        P("dp"),
        P(),
    )
    return jax.shard_map(
        on_device, mesh=mesh, in_specs=in_specs, out_specs=P("dp", "tensor"), check_vma=False
    )
```

time: 180 us -> 128 us (0.71)
  waiting for transfers between devices: 122 us -> 35.8 us
  starting transfers between devices: 7.65 us -> 45.9 us
  matrix products: 27.8 us -> 0 us
  blocking collectives: 0 us -> 23 us
  between operations: 14.1 us -> 0.26 us
  Pallas kernels: 0 us -> 12.5 us
  local copies, waits for them, and re-layouts: 0.18 us -> 8.8 us
  other arithmetic: 7.94 us -> 1.7 us
    all_gather x1 -> x0, waiting for transfers between devices: 59.3 us -> none  [on_device(): full = lax.all_gather(hidden, 'tensor', axis=1, tiled=True)]
    reduce_scatter x1 -> x0, waiting for transfers between devices: 51.8 us -> none  [on_device(): lax.psum_scatter(partial_sum, 'tensor', scatter_dimension=1, tiled=True)]
    ppermute x0 -> x28, starting transfers between devices: none -> 45.9 us  [send(): return lax.ppermute(x, 'tensor', up if go_up else down)]
    ppermute x0 -> x28, waiting for transfers between devices: none -> 35.8 us  [send(): return lax.ppermute(x, 'tensor', up if go_up else down)]
    dot_general x5 -> x0, matrix products: 27.8 us -> none  [the longest x1 7.01 us: attend(): jnp.einsum('qhgd,khd->hgqk', query_part, key_part, preferred_element_type...]
    all_to_all x0 -> x1, blocking collectives: none -> 23 us  [on_device(): lax.all_to_all(leaving, 'dp', split_axis=0, concat_axis=0, tiled=True)]
    pallas_call x0 -> x9, Pallas kernels: none -> 12.5 us  [call(): pl.pallas_call(kernel, out_shape=[jax.ShapeDtypeStruct(shape, BF) for sha...]
    all_to_all x1 -> x0, waiting for transfers between devices: 10.2 us -> none  [on_device(): lax.all_to_all(leaving, 'dp', split_axis=0, concat_axis=0, tiled=True)]
  transfers between devices with their start and end apart: 3 -> 28, of which waited for: 3 -> 12; matrix products, arithmetic and copies ran while one was open for 2% -> 1% of each run, Pallas kernels for 0% -> 5%
where the time goes in v2:
time: 128 us
  starting transfers between devices  45.9 us (36%)
  waiting for transfers between devices  35.8 us (28%)
  blocking collectives  23 us (18%)
  Pallas kernels  12.5 us (10%)
  local copies, waits for them, and re-layouts  8.8 us (7%)
  other arithmetic  1.7 us (1%)
    ppermute x28, starting transfers between devices, send(): return lax.ppermute(x, 'tensor', up if go_up else down)  45.9 us
    ppermute x28, waiting for transfers between devices, send(): return lax.ppermute(x, 'tensor', up if go_up else down)  35.8 us
    all_to_all x1, blocking collectives, on_device(): lax.all_to_all(leaving, 'dp', split_axis=0, concat_axis=0, tiled=True)  23 us
    pallas_call x9, Pallas kernels, call(): pl.pallas_call(kernel, out_shape=[jax.ShapeDtypeStruct(shape, BF) for sha...  12.5 us
    unnamed x18, local copies, waits for them, and re-layouts  7.73 us
  transfers between devices with their start and end apart: 28, of which 12 were waited for; matrix products, arithmetic and copies ran while one was open for 1% of the time, Pallas kernels for 5%

profile of v2, /device:TPU:1, one launch (start us, length us, event | category | flops | bytes accessed | tf_op | source)
XLA Modules:
  0.0 127.9 jit_solution(15473082044728750872)
XLA Ops:
  1.1 6.5 %collective-permute-start.15 = (bf16[256,512]{1,0:T(8,128)(2,1)S(1)}, bf16[256,512]{1,0:T(8,128)(2,1)S(1)}, u32[]{:S(2)}, u32[]{:S(2)}) collective-permute-start(bf16[256,512]{1,0:T(8,128)(2,1)S(1)} %get-tuple-element.55.refs_0_), channel_id=1, source_target_pairs={{0,7},{1,0},{2,1},{3,2},{4,3},{5,4},{6,5},{7,6},{8,15},{9,8},{10,9... | collective-permute-start | bytes 786440 | tf_op jit(solution)/shard_map/ppermute | solution.py:159
  7.6 5.0 %collective-permute-done.15.refs_2_ = bf16[256,512]{1,0:T(8,128)(2,1)S(1)} collective-permute-done((bf16[256,512]{1,0:T(8,128)(2,1)S(1)}, bf16[256,512]{1,0:T(8,128)(2,1)S(1)}, u32[]{:S(2)}, u32[]{:S(2)}) %collective-permute-start.15) | collective-permute-done | bytes 262176 | tf_op jit(solution)/shard_map/ppermute | solution.py:159
  12.5 3.4 %collective-permute-start.17 = (bf16[256,512]{1,0:T(8,128)(2,1)S(1)}, bf16[256,512]{1,0:T(8,128)(2,1)S(1)}, u32[]{:S(2)}, u32[]{:S(2)}) collective-permute-start(bf16[256,512]{1,0:T(8,128)(2,1)S(1)} %collective-permute-done.15.refs_2_), channel_id=1, source_target_pairs={{0,7},{1,0},{2,1},{3,2},{4,3},{5,4},{6,5},{7,6},{8,15},{9,8},{10,9... | collective-permute-start | bytes 786440 | tf_op jit(solution)/shard_map/ppermute | solution.py:159
  16.0 1.4 %collective-permute-start.2 = (bf16[256,512]{1,0:T(8,128)(2,1)S(1)}, bf16[256,512]{1,0:T(8,128)(2,1)S(1)}, u32[]{:S(2)}, u32[]{:S(2)}) collective-permute-start(bf16[256,512]{1,0:T(8,128)(2,1)S(1)} %collective-permute-done.refs_1_), channel_id=1, source_target_pairs={{0,1},{1,2},{2,3},{3,4},{4,5},{5,6},{6,7},{7,0},{8,9},{9,10},{10,1... | collective-permute-start | bytes 786440 | tf_op jit(solution)/shard_map/ppermute | solution.py:159
  17.4 3.9 %collective-permute-done.14.refs_1_ = bf16[256,512]{1,0:T(8,128)(2,1)S(1)} collective-permute-done((bf16[256,512]{1,0:T(8,128)(2,1)S(1)}, bf16[256,512]{1,0:T(8,128)(2,1)S(1)}, u32[]{:S(2)}, u32[]{:S(2)}) %collective-permute-start.14) | collective-permute-done | bytes 262176 | tf_op jit(solution)/shard_map/ppermute | solution.py:159
  21.3 2.7 %collective-permute-start.19 = (bf16[256,512]{1,0:T(8,128)(2,1)S(1)}, bf16[256,512]{1,0:T(8,128)(2,1)S(1)}, u32[]{:S(2)}, u32[]{:S(2)}) collective-permute-start(bf16[256,512]{1,0:T(8,128)(2,1)S(1)} %collective-permute-done.17.refs_4_), channel_id=1, source_target_pairs={{0,7},{1,0},{2,1},{3,2},{4,3},{5,4},{6,5},{7,6},{8,15},{9,8},{10,9... | collective-permute-start | bytes 786440 | tf_op jit(solution)/shard_map/ppermute | solution.py:159
  24.0 1.7 %collective-permute-done.1.refs_2_ = bf16[256,512]{1,0:T(8,128)(2,1)S(1)} collective-permute-done((bf16[256,512]{1,0:T(8,128)(2,1)S(1)}, bf16[256,512]{1,0:T(8,128)(2,1)S(1)}, u32[]{:S(2)}, u32[]{:S(2)}) %collective-permute-start.1) | collective-permute-done | bytes 262176 | tf_op jit(solution)/shard_map/ppermute | solution.py:159
  25.7 3.4 %collective-permute-start.3 = (bf16[256,512]{1,0:T(8,128)(2,1)S(1)}, bf16[256,512]{1,0:T(8,128)(2,1)S(1)}, u32[]{:S(2)}, u32[]{:S(2)}) collective-permute-start(bf16[256,512]{1,0:T(8,128)(2,1)S(1)} %collective-permute-done.1.refs_2_), channel_id=1, source_target_pairs={{0,7},{1,0},{2,1},{3,2},{4,3},{5,4},{6,5},{7,6},{8,15},{9,8},{10,9... | collective-permute-start | bytes 786440 | tf_op jit(solution)/shard_map/ppermute | solution.py:159
  29.1 3.4 %collective-permute-done.16.refs_3_ = bf16[256,512]{1,0:T(8,128)(2,1)S(1)} collective-permute-done((bf16[256,512]{1,0:T(8,128)(2,1)S(1)}, bf16[256,512]{1,0:T(8,128)(2,1)S(1)}, u32[]{:S(2)}, u32[]{:S(2)}) %collective-permute-start.16) | collective-permute-done | bytes 262176 | tf_op jit(solution)/shard_map/ppermute | solution.py:159
  32.5 2.7 %collective-permute-start.20 = (bf16[256,512]{1,0:T(8,128)(2,1)S(1)}, bf16[256,512]{1,0:T(8,128)(2,1)S(1)}, u32[]{:S(2)}, u32[]{:S(2)}) collective-permute-start(bf16[256,512]{1,0:T(8,128)(2,1)S(1)} %collective-permute-done.19.refs_6_), channel_id=1, source_target_pairs={{0,7},{1,0},{2,1},{3,2},{4,3},{5,4},{6,5},{7,6},{8,15},{9,8},{10,9... | collective-permute-start | bytes 786440 | tf_op jit(solution)/shard_map/ppermute | solution.py:159
  35.2 1.7 %collective-permute-done.3.refs_4_ = bf16[256,512]{1,0:T(8,128)(2,1)S(1)} collective-permute-done((bf16[256,512]{1,0:T(8,128)(2,1)S(1)}, bf16[256,512]{1,0:T(8,128)(2,1)S(1)}, u32[]{:S(2)}, u32[]{:S(2)}) %collective-permute-start.3) | collective-permute-done | bytes 262176 | tf_op jit(solution)/shard_map/ppermute | solution.py:159
  36.9 3.4 %collective-permute-start.5 = (bf16[256,512]{1,0:T(8,128)(2,1)S(1)}, bf16[256,512]{1,0:T(8,128)(2,1)S(1)}, u32[]{:S(2)}, u32[]{:S(2)}) collective-permute-start(bf16[256,512]{1,0:T(8,128)(2,1)S(1)} %collective-permute-done.3.refs_4_), channel_id=1, source_target_pairs={{0,7},{1,0},{2,1},{3,2},{4,3},{5,4},{6,5},{7,6},{8,15},{9,8},{10,9... | collective-permute-start | bytes 786440 | tf_op jit(solution)/shard_map/ppermute | solution.py:159
  41.0 1.6 %collective-permute-done.20.refs_7_ = bf16[256,512]{1,0:T(8,128)(2,1)S(1)} collective-permute-done((bf16[256,512]{1,0:T(8,128)(2,1)S(1)}, bf16[256,512]{1,0:T(8,128)(2,1)S(1)}, u32[]{:S(2)}, u32[]{:S(2)}) %collective-permute-start.20) | collective-permute-done | bytes 262176 | tf_op jit(solution)/shard_map/ppermute | solution.py:159
  42.6 2.2 %copy-done.1 = bf16[4096,512]{1,0:T(8,128)(2,1)S(1)} copy-done((bf16[4096,512]{1,0:T(8,128)(2,1)S(1)}, bf16[4096,512]{1,0:T(8,128)(2,1)}, u32[]{:S(2)}) %copy-start.1) | copy-done | bytes 4194328
  47.2 2.5 %shard_map.76 = (bf16[256,512]{1,0:T(8,128)(2,1)S(1)}, bf16[256,128]{1,0:T(8,128)(2,1)S(1)}, bf16[256,128]{1,0:T(8,128)(2,1)S(1)}) custom-call(bf16[256,512]{1,0:T(8,128)(2,1)S(1)} %get-tuple-element.55.refs_0_, bf16[256,512]{1,0:T(8,128)(2,1)S(1)} %collective-permute-done.14.refs_1_, bf16[256,512]{1,0:T(8,128)(2,1)S(1)} %collective-permute-done.15.refs_2_, ...), custom_call_target="tpu_custom_call" | custom-call | tf_op jit(solution)/shard_map/pallas_call | solution.py:139
  50.7 3.4 %shard_map.74 = (bf16[256,512]{1,0:T(8,128)(2,1)S(1)}, bf16[256,128]{1,0:T(8,128)(2,1)S(1)}, bf16[256,128]{1,0:T(8,128)(2,1)S(1)}, bf16[256,512]{1,0:T(8,128)(2,1)S(1)}, bf16[256,512]{1,0:T(8,128)(2,1)S(1)}) custom-call(bf16[256,512]{1,0:T(8,128)(2,1)S(1)} %get-tuple-element.56.refs_0_, bf16[256,512]{1,0:T(8,128)(2,1)S(1)} %collective-permute-done.refs_1_, ...), custom_call_target="tpu_custom_call" | custom-call | tf_op jit(solution)/shard_map/pallas_call | solution.py:139
  54.0 1.7 %shard_map.77 = (bf16[256,512]{1,0:T(8,128)(2,1)S(1)}, bf16[256,512]{1,0:T(8,128)(2,1)S(1)}, bf16[256,512]{1,0:T(8,128)(2,1)S(1)}) custom-call(bf16[256,512]{1,0:T(8,128)(2,1)S(1)} %get-tuple-element.39.q, bf16[256,128]{1,0:T(8,128)(2,1)S(1)} %get-tuple-element.40.k0, bf16[256,128]{1,0:T(8,128)(2,1)S(1)} %get-tuple-element.41.v0, ...), custom_call_target="tpu_custom_call" | custom-call | tf_op jit(solution)/shard_map/pallas_call | solution.py:139
  55.7 3.5 %collective-permute-start.24 = (bf16[256,512]{1,0:T(8,128)(2,1)S(1)}, bf16[256,512]{1,0:T(8,128)(2,1)S(1)}, u32[]{:S(2)}, u32[]{:S(2)}) collective-permute-start(bf16[256,512]{1,0:T(8,128)(2,1)S(1)} %get-tuple-element.52), channel_id=1, source_target_pairs={{0,7},{1,0},{2,1},{3,2},{4,3},{5,4},{6,5},{7,6},{8,15},{9,8},{10,9... | collective-permute-start | bytes 786440 | tf_op jit(solution)/shard_map/ppermute | solution.py:159
  61.2 2.7 %collective-permute-start.11 = (bf16[256,512]{1,0:T(8,128)(2,1)S(1)}, bf16[256,512]{1,0:T(8,128)(2,1)S(1)}, u32[]{:S(2)}, u32[]{:S(2)}) collective-permute-start(bf16[256,512]{1,0:T(8,128)(2,1)S(1)} %get-tuple-element.38), channel_id=1, source_target_pairs={{0,7},{1,0},{2,1},{3,2},{4,3},{5,4},{6,5},{7,6},{8,15},{9,8},{10,9... | collective-permute-start | bytes 786440 | tf_op jit(solution)/shard_map/ppermute | solution.py:159
  64.1 2.7 %collective-permute-start.25 = (bf16[256,512]{1,0:T(8,128)(2,1)S(1)}, bf16[256,512]{1,0:T(8,128)(2,1)S(1)}, u32[]{:S(2)}, u32[]{:S(2)}) collective-permute-start(bf16[256,512]{1,0:T(8,128)(2,1)S(1)} %add_convert_fusion.2), channel_id=1, source_target_pairs={{0,7},{1,0},{2,1},{3,2},{4,3},{5,4},{6,5},{7,6},{8,15},{9,8},{10,9... | collective-permute-start | bytes 786440 | tf_op jit(solution)/shard_map/ppermute | solution.py:159
  67.2 2.8 %collective-permute-done.11 = bf16[256,512]{1,0:T(8,128)(2,1)S(1)} collective-permute-done((bf16[256,512]{1,0:T(8,128)(2,1)S(1)}, bf16[256,512]{1,0:T(8,128)(2,1)S(1)}, u32[]{:S(2)}, u32[]{:S(2)}) %collective-permute-start.11) | collective-permute-done | bytes 262176 | tf_op jit(solution)/shard_map/ppermute | solution.py:159
  70.1 3.5 %collective-permute-start.12 = (bf16[256,512]{1,0:T(8,128)(2,1)S(1)}, bf16[256,512]{1,0:T(8,128)(2,1)S(1)}, u32[]{:S(2)}, u32[]{:S(2)}) collective-permute-start(bf16[256,512]{1,0:T(8,128)(2,1)S(1)} %add_convert_fusion.6), channel_id=1, source_target_pairs={{0,7},{1,0},{2,1},{3,2},{4,3},{5,4},{6,5},{7,6},{8,15},{9,8},{10,9... | collective-permute-start | bytes 786440 | tf_op jit(solution)/shard_map/ppermute | solution.py:159
  73.7 1.9 %collective-permute-done.25 = bf16[256,512]{1,0:T(8,128)(2,1)S(1)} collective-permute-done((bf16[256,512]{1,0:T(8,128)(2,1)S(1)}, bf16[256,512]{1,0:T(8,128)(2,1)S(1)}, u32[]{:S(2)}, u32[]{:S(2)}) %collective-permute-start.25) | collective-permute-done | bytes 262176 | tf_op jit(solution)/shard_map/ppermute | solution.py:159
  75.7 3.5 %collective-permute-start.26 = (bf16[256,512]{1,0:T(8,128)(2,1)S(1)}, bf16[256,512]{1,0:T(8,128)(2,1)S(1)}, u32[]{:S(2)}, u32[]{:S(2)}) collective-permute-start(bf16[256,512]{1,0:T(8,128)(2,1)S(1)} %add_convert_fusion.1), channel_id=1, source_target_pairs={{0,7},{1,0},{2,1},{3,2},{4,3},{5,4},{6,5},{7,6},{8,15},{9,8},{10,9... | collective-permute-start | bytes 786440 | tf_op jit(solution)/shard_map/ppermute | solution.py:159
  79.4 5.0 %collective-permute-done.8 = bf16[256,512]{1,0:T(8,128)(2,1)S(1)} collective-permute-done((bf16[256,512]{1,0:T(8,128)(2,1)S(1)}, bf16[256,512]{1,0:T(8,128)(2,1)S(1)}, u32[]{:S(2)}, u32[]{:S(2)}) %collective-permute-start.8) | collective-permute-done | bytes 262176 | tf_op jit(solution)/shard_map/ppermute | solution.py:159
  84.6 2.7 %collective-permute-start.13 = (bf16[256,512]{1,0:T(8,128)(2,1)S(1)}, bf16[256,512]{1,0:T(8,128)(2,1)S(1)}, u32[]{:S(2)}, u32[]{:S(2)}) collective-permute-start(bf16[256,512]{1,0:T(8,128)(2,1)S(1)} %add_convert_fusion.5), channel_id=1, source_target_pairs={{0,7},{1,0},{2,1},{3,2},{4,3},{5,4},{6,5},{7,6},{8,15},{9,8},{10,9... | collective-permute-start | bytes 786440 | tf_op jit(solution)/shard_map/ppermute | solution.py:159
  87.4 3.0 %collective-permute-start.27 = (bf16[256,512]{1,0:T(8,128)(2,1)S(1)}, bf16[256,512]{1,0:T(8,128)(2,1)S(1)}, u32[]{:S(2)}, u32[]{:S(2)}) collective-permute-start(bf16[256,512]{1,0:T(8,128)(2,1)S(1)} %add_convert_fusion), channel_id=1, source_target_pairs={{0,7},{1,0},{2,1},{3,2},{4,3},{5,4},{6,5},{7,6},{8,15},{9,8},{10,9... | collective-permute-start | bytes 786440 | tf_op jit(solution)/shard_map/ppermute | solution.py:159
  90.4 5.2 %collective-permute-done.9 = bf16[256,512]{1,0:T(8,128)(2,1)S(1)} collective-permute-done((bf16[256,512]{1,0:T(8,128)(2,1)S(1)}, bf16[256,512]{1,0:T(8,128)(2,1)S(1)}, u32[]{:S(2)}, u32[]{:S(2)}) %collective-permute-start.9) | collective-permute-done | bytes 262176 | tf_op jit(solution)/shard_map/ppermute | solution.py:159
  97.9 1.3 %shard_map.73.pick = bf16[512,512]{1,0:T(8,128)(2,1)S(1)} custom-call(s32[32,32]{1,0:T(8,128)S(1)} %copy-done.7), custom_call_target="tpu_custom_call" | custom-call | tf_op jit(solution)/shard_map/pallas_call | solution.py:139
  99.3 2.9 %collective-permute-done.10.up_a = bf16[256,512]{1,0:T(8,128)(2,1)S(1)} collective-permute-done((bf16[256,512]{1,0:T(8,128)(2,1)S(1)}, bf16[256,512]{1,0:T(8,128)(2,1)S(1)}, u32[]{:S(2)}, u32[]{:S(2)}) %collective-permute-start.10) | collective-permute-done | bytes 262176 | tf_op jit(solution)/shard_map/ppermute | solution.py:159
  102.2 1.6 %shard_map.81 = (bf16[512,512]{1,0:T(8,128)(2,1)S(1)}, bf16[512,512]{1,0:T(8,128)(2,1)S(1)}) custom-call(s32[32,32]{1,0:T(8,128)S(1)} %copy-done.7, bf16[512,512]{1,0:T(8,128)(2,1)S(1)} %shard_map.73.pick, bf16[256,512]{1,0:T(8,128)(2,1)S(1)} %get-tuple-element.31.own_a, bf16[256,512]{1,0:T(8,128)(2,1)S(1)} %collective-permute-done.10.up_a, ...), custom_call_target="tpu_custom_call" | custom-call | tf_op jit(solution)/shard_map/pallas_call | solution.py:139
  103.8 23.0 %all_to_all.5 = bf16[32,16,512]{2,1,0:T(8,128)(2,1)S(1)} all-to-all(bf16[32,16,512]{2,1,0:T(8,128)(2,1)S(1)} %bitcast.3), channel_id=1, replica_groups=mesh['dp'=32,'tensor'=8] {'dp'}, dimensions={0} | all-to-all | bytes 1048576 | tf_op jit(solution)/shard_map/all_to_all | solution.py:225
  (64 shorter events, 11.6 us)
Async XLA Ops:
  1.1 48.6 %copy-start.8 = (s32[512]{0:T(512)S(1)}, s32[512]{0:T(512)}, u32[]{:S(2)}) copy-start(s32[512]{0:T(512)} %param.12) | copy-start | bytes 6148
  1.1 11.5 %collective-permute-start.15 = (bf16[256,512]{1,0:T(8,128)(2,1)S(1)}, bf16[256,512]{1,0:T(8,128)(2,1)S(1)}, u32[]{:S(2)}, u32[]{:S(2)}) collective-permute-start(bf16[256,512]{1,0:T(8,128)(2,1)S(1)} %get-tuple-element.55.refs_0_), channel_id=1, source_target_pairs={{0,7},{1,0},{2,1},{3,2},{4,3},{5,4},{6,5},{7,6},{8,15},{9,8},{10,9... | collective-permute-start | bytes 786440 | tf_op jit(solution)/shard_map/ppermute | solution.py:159
  7.5 8.4 %collective-permute-start = (bf16[256,512]{1,0:T(8,128)(2,1)S(1)}, bf16[256,512]{1,0:T(8,128)(2,1)S(1)}, u32[]{:S(2)}, u32[]{:S(2)}) collective-permute-start(bf16[256,512]{1,0:T(8,128)(2,1)S(1)} %get-tuple-element.56.refs_0_), channel_id=1, source_target_pairs={{0,1},{1,2},{2,3},{3,4},{4,5},{5,6},{6,7},{7,0},{8,9},{9,10},{10,1... | collective-permute-start | bytes 786440 | tf_op jit(solution)/shard_map/ppermute | solution.py:159
  7.6 13.7 %collective-permute-start.14 = (bf16[256,512]{1,0:T(8,128)(2,1)S(1)}, bf16[256,512]{1,0:T(8,128)(2,1)S(1)}, u32[]{:S(2)}, u32[]{:S(2)}) collective-permute-start(bf16[256,512]{1,0:T(8,128)(2,1)S(1)} %get-tuple-element.55.refs_0_), channel_id=1, source_target_pairs={{0,1},{1,2},{2,3},{3,4},{4,5},{5,6},{6,7},{7,0},{8,9},{9,10},{10,1... | collective-permute-start | bytes 786440 | tf_op jit(solution)/shard_map/ppermute | solution.py:159
  12.5 8.8 %collective-permute-start.17 = (bf16[256,512]{1,0:T(8,128)(2,1)S(1)}, bf16[256,512]{1,0:T(8,128)(2,1)S(1)}, u32[]{:S(2)}, u32[]{:S(2)}) collective-permute-start(bf16[256,512]{1,0:T(8,128)(2,1)S(1)} %collective-permute-done.15.refs_2_), channel_id=1, source_target_pairs={{0,7},{1,0},{2,1},{3,2},{4,3},{5,4},{6,5},{7,6},{8,15},{9,8},{10,9... | collective-permute-start | bytes 786440 | tf_op jit(solution)/shard_map/ppermute | solution.py:159
  16.0 9.8 %collective-permute-start.1 = (bf16[256,512]{1,0:T(8,128)(2,1)S(1)}, bf16[256,512]{1,0:T(8,128)(2,1)S(1)}, u32[]{:S(2)}, u32[]{:S(2)}) collective-permute-start(bf16[256,512]{1,0:T(8,128)(2,1)S(1)} %get-tuple-element.56.refs_0_), channel_id=1, source_target_pairs={{0,7},{1,0},{2,1},{3,2},{4,3},{5,4},{6,5},{7,6},{8,15},{9,8},{10,9... | collective-permute-start | bytes 786440 | tf_op jit(solution)/shard_map/ppermute | solution.py:159
  16.0 13.1 %collective-permute-start.2 = (bf16[256,512]{1,0:T(8,128)(2,1)S(1)}, bf16[256,512]{1,0:T(8,128)(2,1)S(1)}, u32[]{:S(2)}, u32[]{:S(2)}) collective-permute-start(bf16[256,512]{1,0:T(8,128)(2,1)S(1)} %collective-permute-done.refs_1_), channel_id=1, source_target_pairs={{0,1},{1,2},{2,3},{3,4},{4,5},{5,6},{6,7},{7,0},{8,9},{9,10},{10,1... | collective-permute-start | bytes 786440 | tf_op jit(solution)/shard_map/ppermute | solution.py:159
  21.3 11.2 %collective-permute-start.16 = (bf16[256,512]{1,0:T(8,128)(2,1)S(1)}, bf16[256,512]{1,0:T(8,128)(2,1)S(1)}, u32[]{:S(2)}, u32[]{:S(2)}) collective-permute-start(bf16[256,512]{1,0:T(8,128)(2,1)S(1)} %collective-permute-done.14.refs_1_), channel_id=1, source_target_pairs={{0,1},{1,2},{2,3},{3,4},{4,5},{5,6},{6,7},{7,0},{8,9},{9,10},{10,1... | collective-permute-start | bytes 786440 | tf_op jit(solution)/shard_map/ppermute | solution.py:159
  21.3 11.2 %collective-permute-start.19 = (bf16[256,512]{1,0:T(8,128)(2,1)S(1)}, bf16[256,512]{1,0:T(8,128)(2,1)S(1)}, u32[]{:S(2)}, u32[]{:S(2)}) collective-permute-start(bf16[256,512]{1,0:T(8,128)(2,1)S(1)} %collective-permute-done.17.refs_4_), channel_id=1, source_target_pairs={{0,7},{1,0},{2,1},{3,2},{4,3},{5,4},{6,5},{7,6},{8,15},{9,8},{10,9... | collective-permute-start | bytes 786440 | tf_op jit(solution)/shard_map/ppermute | solution.py:159
  25.7 11.2 %collective-permute-start.3 = (bf16[256,512]{1,0:T(8,128)(2,1)S(1)}, bf16[256,512]{1,0:T(8,128)(2,1)S(1)}, u32[]{:S(2)}, u32[]{:S(2)}) collective-permute-start(bf16[256,512]{1,0:T(8,128)(2,1)S(1)} %collective-permute-done.1.refs_2_), channel_id=1, source_target_pairs={{0,7},{1,0},{2,1},{3,2},{4,3},{5,4},{6,5},{7,6},{8,15},{9,8},{10,9... | collective-permute-start | bytes 786440 | tf_op jit(solution)/shard_map/ppermute | solution.py:159
  29.1 11.2 %collective-permute-start.4 = (bf16[256,512]{1,0:T(8,128)(2,1)S(1)}, bf16[256,512]{1,0:T(8,128)(2,1)S(1)}, u32[]{:S(2)}, u32[]{:S(2)}) collective-permute-start(bf16[256,512]{1,0:T(8,128)(2,1)S(1)} %collective-permute-done.2.refs_3_), channel_id=1, source_target_pairs={{0,1},{1,2},{2,3},{3,4},{4,5},{5,6},{6,7},{7,0},{8,9},{9,10},{10,1... | collective-permute-start | bytes 786440 | tf_op jit(solution)/shard_map/ppermute | solution.py:159
  32.5 8.4 %collective-permute-start.18 = (bf16[256,512]{1,0:T(8,128)(2,1)S(1)}, bf16[256,512]{1,0:T(8,128)(2,1)S(1)}, u32[]{:S(2)}, u32[]{:S(2)}) collective-permute-start(bf16[256,512]{1,0:T(8,128)(2,1)S(1)} %collective-permute-done.16.refs_3_), channel_id=1, source_target_pairs={{0,1},{1,2},{2,3},{3,4},{4,5},{5,6},{6,7},{7,0},{8,9},{9,10},{10,1... | collective-permute-start | bytes 786440 | tf_op jit(solution)/shard_map/ppermute | solution.py:159
  32.5 10.0 %collective-permute-start.20 = (bf16[256,512]{1,0:T(8,128)(2,1)S(1)}, bf16[256,512]{1,0:T(8,128)(2,1)S(1)}, u32[]{:S(2)}, u32[]{:S(2)}) collective-permute-start(bf16[256,512]{1,0:T(8,128)(2,1)S(1)} %collective-permute-done.19.refs_6_), channel_id=1, source_target_pairs={{0,7},{1,0},{2,1},{3,2},{4,3},{5,4},{6,5},{7,6},{8,15},{9,8},{10,9... | collective-permute-start | bytes 786440 | tf_op jit(solution)/shard_map/ppermute | solution.py:159
  36.9 12.7 %collective-permute-start.5 = (bf16[256,512]{1,0:T(8,128)(2,1)S(1)}, bf16[256,512]{1,0:T(8,128)(2,1)S(1)}, u32[]{:S(2)}, u32[]{:S(2)}) collective-permute-start(bf16[256,512]{1,0:T(8,128)(2,1)S(1)} %collective-permute-done.3.refs_4_), channel_id=1, source_target_pairs={{0,7},{1,0},{2,1},{3,2},{4,3},{5,4},{6,5},{7,6},{8,15},{9,8},{10,9... | collective-permute-start | bytes 786440 | tf_op jit(solution)/shard_map/ppermute | solution.py:159
  40.4 9.3 %collective-permute-start.6 = (bf16[256,512]{1,0:T(8,128)(2,1)S(1)}, bf16[256,512]{1,0:T(8,128)(2,1)S(1)}, u32[]{:S(2)}, u32[]{:S(2)}) collective-permute-start(bf16[256,512]{1,0:T(8,128)(2,1)S(1)} %collective-permute-done.4.refs_5_), channel_id=1, source_target_pairs={{0,1},{1,2},{2,3},{3,4},{4,5},{5,6},{6,7},{7,0},{8,9},{9,10},{10,1... | collective-permute-start | bytes 786440 | tf_op jit(solution)/shard_map/ppermute | solution.py:159
  42.6 2.2 %copy-start.1 = (bf16[4096,512]{1,0:T(8,128)(2,1)S(1)}, bf16[4096,512]{1,0:T(8,128)(2,1)}, u32[]{:S(2)}) copy-start(bf16[4096,512]{1,0:T(8,128)(2,1)} %refs_1_.2) | copy-start | bytes 12582916
  47.2 2.5 %copy-start = (bf16[512,4096]{1,0:T(8,128)(2,1)S(1)}, bf16[512,4096]{1,0:T(8,128)(2,1)}, u32[]{:S(2)}) copy-start(bf16[512,4096]{1,0:T(8,128)(2,1)} %refs_0_.2) | copy-start | bytes 12582916
  47.2 3.5 %copy-start.2 = (bf16[4096,512]{1,0:T(8,128)(2,1)S(1)}, bf16[4096,512]{1,0:T(8,128)(2,1)}, u32[]{:S(2)}) copy-start(bf16[4096,512]{1,0:T(8,128)(2,1)} %refs_1_.2) | copy-start | bytes 12582916
  55.7 8.2 %collective-permute-start.24 = (bf16[256,512]{1,0:T(8,128)(2,1)S(1)}, bf16[256,512]{1,0:T(8,128)(2,1)S(1)}, u32[]{:S(2)}, u32[]{:S(2)}) collective-permute-start(bf16[256,512]{1,0:T(8,128)(2,1)S(1)} %get-tuple-element.52), channel_id=1, source_target_pairs={{0,7},{1,0},{2,1},{3,2},{4,3},{5,4},{6,5},{7,6},{8,15},{9,8},{10,9... | collective-permute-start | bytes 786440 | tf_op jit(solution)/shard_map/ppermute | solution.py:159
  59.2 7.6 %collective-permute-start.21 = (bf16[256,512]{1,0:T(8,128)(2,1)S(1)}, bf16[256,512]{1,0:T(8,128)(2,1)S(1)}, u32[]{:S(2)}, u32[]{:S(2)}) collective-permute-start(bf16[256,512]{1,0:T(8,128)(2,1)S(1)} %get-tuple-element.48), channel_id=1, source_target_pairs={{0,1},{1,2},{2,3},{3,4},{4,5},{5,6},{6,7},{7,0},{8,9},{9,10},{10,1... | collective-permute-start | bytes 786440 | tf_op jit(solution)/shard_map/ppermute | solution.py:159
  61.2 8.8 %collective-permute-start.11 = (bf16[256,512]{1,0:T(8,128)(2,1)S(1)}, bf16[256,512]{1,0:T(8,128)(2,1)S(1)}, u32[]{:S(2)}, u32[]{:S(2)}) collective-permute-start(bf16[256,512]{1,0:T(8,128)(2,1)S(1)} %get-tuple-element.38), channel_id=1, source_target_pairs={{0,7},{1,0},{2,1},{3,2},{4,3},{5,4},{6,5},{7,6},{8,15},{9,8},{10,9... | collective-permute-start | bytes 786440 | tf_op jit(solution)/shard_map/ppermute | solution.py:159
  64.0 9.6 %collective-permute-start.7 = (bf16[256,512]{1,0:T(8,128)(2,1)S(1)}, bf16[256,512]{1,0:T(8,128)(2,1)S(1)}, u32[]{:S(2)}, u32[]{:S(2)}) collective-permute-start(bf16[256,512]{1,0:T(8,128)(2,1)S(1)} %get-tuple-element.35), channel_id=1, source_target_pairs={{0,1},{1,2},{2,3},{3,4},{4,5},{5,6},{6,7},{7,0},{8,9},{9,10},{10,1... | collective-permute-start | bytes 786440 | tf_op jit(solution)/shard_map/ppermute | solution.py:159
  64.1 11.6 %collective-permute-start.25 = (bf16[256,512]{1,0:T(8,128)(2,1)S(1)}, bf16[256,512]{1,0:T(8,128)(2,1)S(1)}, u32[]{:S(2)}, u32[]{:S(2)}) collective-permute-start(bf16[256,512]{1,0:T(8,128)(2,1)S(1)} %add_convert_fusion.2), channel_id=1, source_target_pairs={{0,7},{1,0},{2,1},{3,2},{4,3},{5,4},{6,5},{7,6},{8,15},{9,8},{10,9... | collective-permute-start | bytes 786440 | tf_op jit(solution)/shard_map/ppermute | solution.py:159
  66.9 12.3 %collective-permute-start.22 = (bf16[256,512]{1,0:T(8,128)(2,1)S(1)}, bf16[256,512]{1,0:T(8,128)(2,1)S(1)}, u32[]{:S(2)}, u32[]{:S(2)}) collective-permute-start(bf16[256,512]{1,0:T(8,128)(2,1)S(1)} %add_convert_fusion.4), channel_id=1, source_target_pairs={{0,1},{1,2},{2,3},{3,4},{4,5},{5,6},{6,7},{7,0},{8,9},{9,10},{10,1... | collective-permute-start | bytes 786440 | tf_op jit(solution)/shard_map/ppermute | solution.py:159
  70.1 14.5 %collective-permute-start.12 = (bf16[256,512]{1,0:T(8,128)(2,1)S(1)}, bf16[256,512]{1,0:T(8,128)(2,1)S(1)}, u32[]{:S(2)}, u32[]{:S(2)}) collective-permute-start(bf16[256,512]{1,0:T(8,128)(2,1)S(1)} %add_convert_fusion.6), channel_id=1, source_target_pairs={{0,7},{1,0},{2,1},{3,2},{4,3},{5,4},{6,5},{7,6},{8,15},{9,8},{10,9... | collective-permute-start | bytes 786440 | tf_op jit(solution)/shard_map/ppermute | solution.py:159
  73.6 10.7 %collective-permute-start.8 = (bf16[256,512]{1,0:T(8,128)(2,1)S(1)}, bf16[256,512]{1,0:T(8,128)(2,1)S(1)}, u32[]{:S(2)}, u32[]{:S(2)}) collective-permute-start(bf16[256,512]{1,0:T(8,128)(2,1)S(1)} %add_convert_fusion.9), channel_id=1, source_target_pairs={{0,1},{1,2},{2,3},{3,4},{4,5},{5,6},{6,7},{7,0},{8,9},{9,10},{10,1... | collective-permute-start | bytes 786440 | tf_op jit(solution)/shard_map/ppermute | solution.py:159
  75.7 11.7 %collective-permute-start.26 = (bf16[256,512]{1,0:T(8,128)(2,1)S(1)}, bf16[256,512]{1,0:T(8,128)(2,1)S(1)}, u32[]{:S(2)}, u32[]{:S(2)}) collective-permute-start(bf16[256,512]{1,0:T(8,128)(2,1)S(1)} %add_convert_fusion.1), channel_id=1, source_target_pairs={{0,7},{1,0},{2,1},{3,2},{4,3},{5,4},{6,5},{7,6},{8,15},{9,8},{10,9... | collective-permute-start | bytes 786440 | tf_op jit(solution)/shard_map/ppermute | solution.py:159
  79.3 20.1 %collective-permute-start.23 = (bf16[256,512]{1,0:T(8,128)(2,1)S(1)}, bf16[256,512]{1,0:T(8,128)(2,1)S(1)}, u32[]{:S(2)}, u32[]{:S(2)}) collective-permute-start(bf16[256,512]{1,0:T(8,128)(2,1)S(1)} %add_convert_fusion.3), channel_id=1, source_target_pairs={{0,1},{1,2},{2,3},{3,4},{4,5},{5,6},{6,7},{7,0},{8,9},{9,10},{10,1... | collective-permute-start | bytes 786440 | tf_op jit(solution)/shard_map/ppermute | solution.py:159
  84.4 11.2 %collective-permute-start.9 = (bf16[256,512]{1,0:T(8,128)(2,1)S(1)}, bf16[256,512]{1,0:T(8,128)(2,1)S(1)}, u32[]{:S(2)}, u32[]{:S(2)}) collective-permute-start(bf16[256,512]{1,0:T(8,128)(2,1)S(1)} %add_convert_fusion.8), channel_id=1, source_target_pairs={{0,1},{1,2},{2,3},{3,4},{4,5},{5,6},{6,7},{7,0},{8,9},{9,10},{10,1... | collective-permute-start | bytes 786440 | tf_op jit(solution)/shard_map/ppermute | solution.py:159
  84.6 14.7 %collective-permute-start.13 = (bf16[256,512]{1,0:T(8,128)(2,1)S(1)}, bf16[256,512]{1,0:T(8,128)(2,1)S(1)}, u32[]{:S(2)}, u32[]{:S(2)}) collective-permute-start(bf16[256,512]{1,0:T(8,128)(2,1)S(1)} %add_convert_fusion.5), channel_id=1, source_target_pairs={{0,7},{1,0},{2,1},{3,2},{4,3},{5,4},{6,5},{7,6},{8,15},{9,8},{10,9... | collective-permute-start | bytes 786440 | tf_op jit(solution)/shard_map/ppermute | solution.py:159
  87.4 11.9 %collective-permute-start.27 = (bf16[256,512]{1,0:T(8,128)(2,1)S(1)}, bf16[256,512]{1,0:T(8,128)(2,1)S(1)}, u32[]{:S(2)}, u32[]{:S(2)}) collective-permute-start(bf16[256,512]{1,0:T(8,128)(2,1)S(1)} %add_convert_fusion), channel_id=1, source_target_pairs={{0,7},{1,0},{2,1},{3,2},{4,3},{5,4},{6,5},{7,6},{8,15},{9,8},{10,9... | collective-permute-start | bytes 786440 | tf_op jit(solution)/shard_map/ppermute | solution.py:159
  95.7 6.5 %collective-permute-start.10 = (bf16[256,512]{1,0:T(8,128)(2,1)S(1)}, bf16[256,512]{1,0:T(8,128)(2,1)S(1)}, u32[]{:S(2)}, u32[]{:S(2)}) collective-permute-start(bf16[256,512]{1,0:T(8,128)(2,1)S(1)} %add_convert_fusion.7), channel_id=1, source_target_pairs={{0,1},{1,2},{2,3},{3,4},{4,5},{5,6},{6,7},{7,0},{8,9},{9,10},{10,1... | collective-permute-start | bytes 786440 | tf_op jit(solution)/shard_map/ppermute | solution.py:159
  (5 other events, 5.9 us)

commit v3 on v2

--- a/solution.py
+++ b/solution.py
@@ -28,14 +28,25 @@
     return pl.multiple_of(lax.rem(me + (offset + n_ring), n_ring) * width, width)
 
 
-def project_in(shards, wq, wk, wv, x):
-    n_ring = len(shards)
+def early_kernel(n_ring, wq, wk, wv, *refs):
+    shards = refs[: n_ring - 1]
+    q, k, v, x = refs[n_ring - 1 :]
     width = shards[0].shape[1]
-    for shard, off in zip(shards, ring_offsets(n_ring)):
+    *near, far = ring_offsets(n_ring)
+    x[:, pl.ds(block_start(far, n_ring, width), width)] = jnp.zeros(shards[0].shape, BF)
+    for shard, off in zip(shards, near):
         x[:, pl.ds(block_start(off, n_ring, width), width)] = shard[...]
     rows = x[...]
+    for out, w in zip((q, k, v), (wq, wk, wv)):
+        out[...] = jnp.dot(rows, w[...], preferred_element_type=F32)
+
+
+def finish_in(n_ring, far, parts, weights):
+    width = far.shape[1]
+    at = pl.ds(block_start(n_ring // 2, n_ring, width), width)
     return tuple(
-        jnp.dot(rows, w[...], preferred_element_type=F32).astype(BF) for w in (wq, wk, wv)
+        (part[...] + jnp.dot(far[...], w[at, :], preferred_element_type=F32)).astype(BF)
+        for part, w in zip(parts, weights)
     )
 
 
@@ -69,40 +80,34 @@
         out[...] = jnp.dot(mixed, block, preferred_element_type=F32).astype(BF)
 
 
-def first_kernel(n_ring, offsets, base, *refs):
-    shards = refs[:n_ring]
-    wq, wk, wv, wo, ids, mixed_out, k_out, v_out, *outs, x = refs[n_ring:]
-    query, key, value = project_in(shards, wq, wk, wv, x)
+def first_kernel(n_ring, offsets, far, q, k, v, wq, wk, wv, wo, ids, mixed_out, k_out, v_out, *outs):
+    query, key, value = finish_in(n_ring, far, (q, k, v), (wq, wk, wv))
     k_out[...] = key
     v_out[...] = value
-    mixed = attend(query, key, value, ids, base)
+    mixed = attend(query, key, value, ids, 0)
     mixed_out[...] = mixed
     project_out(mixed, wo, offsets, n_ring, outs)
 
 
-def qkv_kernel(n_ring, offsets, base, *refs):
-    shards = refs[:n_ring]
-    wq, wk, wv, q_out, k_out, v_out, x = refs[n_ring:]
-    q_out[...], k_out[...], v_out[...] = project_in(shards, wq, wk, wv, x)
-
-
-def attend_kernel(n_ring, offsets, base, q, k0, v0, k1, v1, wo, ids, mixed_out, *outs):
-    key = jnp.concatenate([k0[...], k1[...]], axis=0)
-    value = jnp.concatenate([v0[...], v1[...]], axis=0)
-    mixed = attend(q[...], key, value, ids, base)
+def second_kernel(n_ring, offsets, far, q, k, v, k0, v0, wq, wk, wv, wo, ids, mixed_out, *outs):
+    query, key, value = finish_in(n_ring, far, (q, k, v), (wq, wk, wv))
+    key = jnp.concatenate([k0[...], key], axis=0)
+    value = jnp.concatenate([v0[...], value], axis=0)
+    mixed = attend(query, key, value, ids, k0.shape[0])
     mixed_out[...] = mixed
     project_out(mixed, wo, offsets, n_ring, outs)
 
 
-def rest_kernel(n_ring, offsets, base, mixed, wo, *outs):
+def rest_kernel(n_ring, offsets, mixed, wo, *outs):
     project_out(mixed[...], wo, offsets, n_ring, outs)
 
 
-def plan_kernel(counts, pick):
+def plan_kernel(counts, pick, stay):
     peers = counts.shape[1]
     rows = pick.shape[1]
     me = lax.axis_index("dp")
     start = rows - lax.fori_loop(0, peers, lambda j, n: n + counts[me, j], 0)
+    stay[...] = (lax.broadcasted_iota(jnp.int32, stay.shape, 0) < start).astype(F32).astype(BF)
     slot = lax.broadcasted_iota(jnp.int32, (SLOT, rows), 0)
     gap = lax.broadcasted_iota(jnp.int32, (SLOT, rows), 1) - slot
 
@@ -120,25 +125,24 @@
     refs[-1][...] = jnp.zeros(refs[-1].shape, BF)
 
 
-def finish_kernel(counts, pick, own_a, up_a, down_a, own_b, up_b, down_b, *refs):
-    *_, leaving, home = refs
-    total_a = own_a[...].astype(F32) + up_a[...].astype(F32) + down_a[...].astype(F32)
-    total_b = own_b[...].astype(F32) + up_b[...].astype(F32) + down_b[...].astype(F32)
-    done = jnp.concatenate([total_a, total_b], axis=0)
-    leaving[...] = jnp.dot(pick[...], done.astype(BF), preferred_element_type=F32).astype(BF)
+def finish_kernel(low, pick, stay, own, up, down, *refs):
+    *before, leaving, home = refs
+    done = own[...].astype(F32) + up[...].astype(F32) + down[...].astype(F32)
     rows = done.shape[0]
-    me = lax.axis_index("dp")
-    kept = rows - lax.fori_loop(0, counts.shape[1], lambda j, n: n + counts[me, j], 0)
-    row = lax.broadcasted_iota(jnp.int32, done.shape, 0)
-    home[...] = jnp.where(row < kept, done, 0.0).astype(BF)
-
-
-def call(kernel, operands, outs, scratch=(), scalars=0):
+    picked = jnp.dot(pick[:, low : low + rows], done.astype(BF), preferred_element_type=F32)
+    if before:
+        picked = picked + before[0][...].astype(F32)
+    leaving[...] = picked.astype(BF)
+    kept = jnp.concatenate([stay[low : low + rows, :].astype(F32)] * (done.shape[1] // HD), axis=1)
+    home[...] = jnp.where(kept > 0.0, done, 0.0).astype(BF)
+
+
+def call(kernel, operands, outs, scratch=(), scalars=0, kind=BF):
     vmem = pl.BlockSpec(memory_space=pltpu.VMEM)
     smem = pl.BlockSpec(memory_space=pltpu.SMEM)
     return pl.pallas_call(
         kernel,
-        out_shape=[jax.ShapeDtypeStruct(shape, BF) for shape in outs],
+        out_shape=[jax.ShapeDtypeStruct(shape, kind) for shape in outs],
         in_specs=[smem] * scalars + [vmem] * (len(operands) - scalars),
         out_specs=[vmem] * len(outs),
         scratch_shapes=scratch,
@@ -185,7 +189,7 @@
 
     w_in = (w_query, w_key, w_value)
     ids = doc_ids[None, :]
-    (pick,) = call(plan_kernel, (send_counts,), [(peers * SLOT, rows)], scalars=1)
+    pick, stay = call(plan_kernel, (send_counts,), [(peers * SLOT, rows), (rows, HD)], scalars=1)
     (mark_out,) = call(touch_kernel, (w_out, w_query), [(SLOT, HD)])
     (mark_in,) = call(touch_kernel, (w_key, w_value), [(SLOT, HD)])
     shards_a = gather(hidden[:cut], True)
@@ -196,34 +200,56 @@
     late_a = tuple(o for o in order if o not in lead_a)
     late_b = tuple(o for o in order if o not in lead_b)
 
-    def body(kernel, offsets=(), base=0):
-        return functools.partial(kernel, n_ring, offsets, base)
-
+    pick, stay = call(plan_kernel, (send_counts,), [(peers * SLOT, rows), (rows, HD)], scalars=1)
+    (mark_out,) = call(touch_kernel, (w_out, w_query), [(SLOT, HD)])
+    (mark_in,) = call(touch_kernel, (w_key, w_value), [(SLOT, HD)])
+    shards_a = gather(hidden[:cut], True)
+    shards_b = gather(hidden[cut:], False)
+    order = ring_offsets(n_ring)[::-1]
+    tile_a, tile_b, kv_a, kv_b = (cut, width), (rows - cut, width), (cut, kv), (rows - cut, kv)
+    lead_a, lead_b = (order[0], order[2]), (order[0], order[1])
+    late_a = tuple(o for o in order if o not in lead_a)
+    late_b = tuple(o for o in order if o not in lead_b)
+
+    def early(shards, tile, kv_tile):
+        return call(
+            functools.partial(early_kernel, n_ring), (*w_in, *shards[:-1]),
+            [tile, kv_tile, kv_tile], [pltpu.VMEM((tile[0], n_ring * width), BF)], kind=F32,
+        )
+
+    def rest(mixed, tile, offsets):
+        return call(
+            functools.partial(rest_kernel, n_ring, offsets), (mixed, w_out),
+            [tile] * len(offsets),
+        )
+
+    early_a = early(shards_a, tile_a, kv_a)
+    early_b = early(shards_b, tile_b, kv_b)
     mixed_a, key_a, value_a, *first_a = call(
-        body(first_kernel, lead_a), (*shards_a, *w_in, w_out, ids),
-        [tile_a, kv_a, kv_a, tile_a, tile_a], [pltpu.VMEM((cut, n_ring * width), BF)],
-    )
-    rest_a = call(body(rest_kernel, late_a), (mixed_a, w_out), [tile_a] * len(late_a))
-    query_b, key_b, value_b = call(
-        body(qkv_kernel), (*shards_b, *w_in), [tile_b, kv_b, kv_b],
-        [pltpu.VMEM((rows - cut, n_ring * width), BF)],
+        functools.partial(first_kernel, n_ring, lead_a),
+        (shards_a[-1], *early_a, *w_in, w_out, ids), [tile_a, kv_a, kv_a, tile_a, tile_a],
     )
     mixed_b, *first_b = call(
-        body(attend_kernel, lead_b, cut),
-        (query_b, key_a, value_a, key_b, value_b, w_out, ids), [tile_b] * 3,
-    )
-    rest_b = call(body(rest_kernel, late_b), (mixed_b, w_out), [tile_b] * len(late_b))
+        functools.partial(second_kernel, n_ring, lead_b),
+        (shards_b[-1], *early_b, key_a, value_a, *w_in, w_out, ids), [tile_b] * 3,
+    )
+    rest_a = rest(mixed_a, tile_a, late_a)
+    rest_b = rest(mixed_b, tile_b, late_b)
     parts_a = dict(zip(lead_a + late_a, [*first_a, *rest_a]))
     parts_b = dict(zip(lead_b + late_b, [*first_b, *rest_b]))
     sums_a = reduce([parts_a[o] for o in order], True)
     sums_b = reduce([parts_b[o] for o in order], False)
-    leaving, home = call(
-        finish_kernel, (send_counts, pick, *sums_a, *sums_b, mark_out, mark_in),
-        [(peers * SLOT, width), (rows, width)], scalars=1,
+    slots = (peers * SLOT, width)
+    leaving, home_a = call(
+        functools.partial(finish_kernel, 0), (pick, stay, *sums_a), [slots, tile_a]
+    )
+    leaving, home_b = call(
+        functools.partial(finish_kernel, cut),
+        (pick, stay, *sums_b, leaving, mark_out, mark_in), [slots, tile_b],
     )
     leaving = leaving.reshape(peers, SLOT, width)
     arrived = lax.all_to_all(leaving, "dp", split_axis=0, concat_axis=0, tiled=True)
-    return jnp.concatenate([home, arrived.reshape(peers * SLOT, width)], axis=0)
+    return jnp.concatenate([home_a, home_b, arrived.reshape(peers * SLOT, width)], axis=0)
 
 
 def solution(mesh):

time: 128 us -> 121 us (0.945)
  starting transfers between devices: 45.9 us -> 41.5 us
  local copies, waits for them, and re-layouts: 8.8 us -> 6.43 us
    ppermute x28, starting transfers between devices: 45.9 us -> 41.5 us  [send(): return lax.ppermute(x, 'tensor', up if go_up else down)]
    unnamed x18, local copies, waits for them, and re-layouts: 7.73 us -> 5.37 us
    pallas_call x9 -> x11, Pallas kernels: 12.5 us -> 12.6 us  [call(): pl.pallas_call(kernel, out_shape=[jax.ShapeDtypeStruct(shape, kind) for s...]
  transfers between devices with their start and end apart: 28 -> 28, of which waited for: 12 -> 13; matrix products, arithmetic and copies ran while one was open for 1% -> 1% of each run, Pallas kernels for 5% -> 8%
where the time goes in v3:
time: 121 us
  starting transfers between devices  41.5 us (34%)
  waiting for transfers between devices  35.7 us (30%)
  blocking collectives  22.2 us (18%)
  Pallas kernels  12.6 us (10%)
  local copies, waits for them, and re-layouts  6.43 us (5%)
  other arithmetic  1.7 us (1%)
    ppermute x28, starting transfers between devices, send(): return lax.ppermute(x, 'tensor', up if go_up else down)  41.5 us
    ppermute x28, waiting for transfers between devices, send(): return lax.ppermute(x, 'tensor', up if go_up else down)  35.7 us
    all_to_all x1, blocking collectives, on_device(): lax.all_to_all(leaving, 'dp', split_axis=0, concat_axis=0, tiled=True)  22.2 us
    pallas_call x11, Pallas kernels, call(): pl.pallas_call(kernel, out_shape=[jax.ShapeDtypeStruct(shape, kind) for s...  12.6 us
    unnamed x18, local copies, waits for them, and re-layouts  5.37 us
  transfers between devices with their start and end apart: 28, of which 13 were waited for; matrix products, arithmetic and copies ran while one was open for 1% of the time, Pallas kernels for 8%

profile of v3, /device:TPU:1, one launch (start us, length us, event | category | flops | bytes accessed | tf_op | source)
XLA Modules:
  0.0 120.5 jit_solution(3982724536524002563)
XLA Ops:
  1.1 2.5 %collective-permute-start = (bf16[256,512]{1,0:T(8,128)(2,1)S(1)}, bf16[256,512]{1,0:T(8,128)(2,1)S(1)}, u32[]{:S(2)}, u32[]{:S(2)}) collective-permute-start(bf16[256,512]{1,0:T(8,128)(2,1)S(1)} %get-tuple-element.69.refs_0_), channel_id=1, source_target_pairs={{0,1},{1,2},{2,3},{3,4},{4,5},{5,6},{6,7},{7,0},{8,9},{9,10},{10,1... | collective-permute-start | bytes 786440 | tf_op jit(solution)/shard_map/ppermute | solution.py:163
  3.6 4.0 %collective-permute-start.14 = (bf16[256,512]{1,0:T(8,128)(2,1)S(1)}, bf16[256,512]{1,0:T(8,128)(2,1)S(1)}, u32[]{:S(2)}, u32[]{:S(2)}) collective-permute-start(bf16[256,512]{1,0:T(8,128)(2,1)S(1)} %get-tuple-element.70.refs_0_), channel_id=1, source_target_pairs={{0,7},{1,0},{2,1},{3,2},{4,3},{5,4},{6,5},{7,6},{8,15},{9,8},{10,9... | collective-permute-start | bytes 786440 | tf_op jit(solution)/shard_map/ppermute | solution.py:163
  7.6 1.4 %collective-permute-start.4 = (bf16[256,512]{1,0:T(8,128)(2,1)S(1)}, bf16[256,512]{1,0:T(8,128)(2,1)S(1)}, u32[]{:S(2)}, u32[]{:S(2)}) collective-permute-start(bf16[256,512]{1,0:T(8,128)(2,1)S(1)} %get-tuple-element.69.refs_0_), channel_id=1, source_target_pairs={{0,7},{1,0},{2,1},{3,2},{4,3},{5,4},{6,5},{7,6},{8,15},{9,8},{10,9... | collective-permute-start | bytes 786440 | tf_op jit(solution)/shard_map/ppermute | solution.py:163
  9.1 4.5 %collective-permute-done.refs_1_ = bf16[256,512]{1,0:T(8,128)(2,1)S(1)} collective-permute-done((bf16[256,512]{1,0:T(8,128)(2,1)S(1)}, bf16[256,512]{1,0:T(8,128)(2,1)S(1)}, u32[]{:S(2)}, u32[]{:S(2)}) %collective-permute-start) | collective-permute-done | bytes 262176 | tf_op jit(solution)/shard_map/ppermute | solution.py:163
  13.6 2.7 %collective-permute-start.15 = (bf16[256,512]{1,0:T(8,128)(2,1)S(1)}, bf16[256,512]{1,0:T(8,128)(2,1)S(1)}, u32[]{:S(2)}, u32[]{:S(2)}) collective-permute-start(bf16[256,512]{1,0:T(8,128)(2,1)S(1)} %collective-permute-done.14.refs_2_), channel_id=1, source_target_pairs={{0,7},{1,0},{2,1},{3,2},{4,3},{5,4},{6,5},{7,6},{8,15},{9,8},{10,9... | collective-permute-start | bytes 786440 | tf_op jit(solution)/shard_map/ppermute | solution.py:163
  16.2 2.0 %collective-permute-done.4.refs_2_ = bf16[256,512]{1,0:T(8,128)(2,1)S(1)} collective-permute-done((bf16[256,512]{1,0:T(8,128)(2,1)S(1)}, bf16[256,512]{1,0:T(8,128)(2,1)S(1)}, u32[]{:S(2)}, u32[]{:S(2)}) %collective-permute-start.4) | collective-permute-done | bytes 262176 | tf_op jit(solution)/shard_map/ppermute | solution.py:163
  18.2 3.4 %collective-permute-start.5 = (bf16[256,512]{1,0:T(8,128)(2,1)S(1)}, bf16[256,512]{1,0:T(8,128)(2,1)S(1)}, u32[]{:S(2)}, u32[]{:S(2)}) collective-permute-start(bf16[256,512]{1,0:T(8,128)(2,1)S(1)} %collective-permute-done.4.refs_2_), channel_id=1, source_target_pairs={{0,7},{1,0},{2,1},{3,2},{4,3},{5,4},{6,5},{7,6},{8,15},{9,8},{10,9... | collective-permute-start | bytes 786440 | tf_op jit(solution)/shard_map/ppermute | solution.py:163
  21.7 3.1 %collective-permute-done.1.refs_3_ = bf16[256,512]{1,0:T(8,128)(2,1)S(1)} collective-permute-done((bf16[256,512]{1,0:T(8,128)(2,1)S(1)}, bf16[256,512]{1,0:T(8,128)(2,1)S(1)}, u32[]{:S(2)}, u32[]{:S(2)}) %collective-permute-start.1) | collective-permute-done | bytes 262176 | tf_op jit(solution)/shard_map/ppermute | solution.py:163
  24.8 2.7 %collective-permute-start.16 = (bf16[256,512]{1,0:T(8,128)(2,1)S(1)}, bf16[256,512]{1,0:T(8,128)(2,1)S(1)}, u32[]{:S(2)}, u32[]{:S(2)}) collective-permute-start(bf16[256,512]{1,0:T(8,128)(2,1)S(1)} %collective-permute-done.15.refs_4_), channel_id=1, source_target_pairs={{0,7},{1,0},{2,1},{3,2},{4,3},{5,4},{6,5},{7,6},{8,15},{9,8},{10,9... | collective-permute-start | bytes 786440 | tf_op jit(solution)/shard_map/ppermute | solution.py:163
  27.5 2.0 %collective-permute-done.5.refs_4_ = bf16[256,512]{1,0:T(8,128)(2,1)S(1)} collective-permute-done((bf16[256,512]{1,0:T(8,128)(2,1)S(1)}, bf16[256,512]{1,0:T(8,128)(2,1)S(1)}, u32[]{:S(2)}, u32[]{:S(2)}) %collective-permute-start.5) | collective-permute-done | bytes 262176 | tf_op jit(solution)/shard_map/ppermute | solution.py:163
  29.5 3.4 %collective-permute-start.6 = (bf16[256,512]{1,0:T(8,128)(2,1)S(1)}, bf16[256,512]{1,0:T(8,128)(2,1)S(1)}, u32[]{:S(2)}, u32[]{:S(2)}) collective-permute-start(bf16[256,512]{1,0:T(8,128)(2,1)S(1)} %collective-permute-done.5.refs_4_), channel_id=1, source_target_pairs={{0,7},{1,0},{2,1},{3,2},{4,3},{5,4},{6,5},{7,6},{8,15},{9,8},{10,9... | collective-permute-start | bytes 786440 | tf_op jit(solution)/shard_map/ppermute | solution.py:163
  35.1 3.4 %collective-permute-start.17 = (bf16[256,512]{1,0:T(8,128)(2,1)S(1)}, bf16[256,512]{1,0:T(8,128)(2,1)S(1)}, u32[]{:S(2)}, u32[]{:S(2)}) collective-permute-start(bf16[256,512]{1,0:T(8,128)(2,1)S(1)} %collective-permute-done.16.refs_6_), channel_id=1, source_target_pairs={{0,7},{1,0},{2,1},{3,2},{4,3},{5,4},{6,5},{7,6},{8,15},{9,8},{10,9... | collective-permute-start | bytes 786440 | tf_op jit(solution)/shard_map/ppermute | solution.py:163
  38.5 2.2 %collective-permute-done.6.refs_6_ = bf16[256,512]{1,0:T(8,128)(2,1)S(1)} collective-permute-done((bf16[256,512]{1,0:T(8,128)(2,1)S(1)}, bf16[256,512]{1,0:T(8,128)(2,1)S(1)}, u32[]{:S(2)}, u32[]{:S(2)}) %collective-permute-start.6) | collective-permute-done | bytes 262176 | tf_op jit(solution)/shard_map/ppermute | solution.py:163
  40.7 2.2 %copy-done = bf16[4096,512]{1,0:T(8,128)(2,1)S(1)} copy-done((bf16[4096,512]{1,0:T(8,128)(2,1)S(1)}, bf16[4096,512]{1,0:T(8,128)(2,1)}, u32[]{:S(2)}) %copy-start) | copy-done | bytes 4194328
  42.9 1.2 %copy-done.3 = bf16[4096,128]{1,0:T(8,128)(2,1)S(1)} copy-done((bf16[4096,128]{1,0:T(8,128)(2,1)S(1)}, bf16[4096,128]{1,0:T(8,128)(2,1)}, u32[]{:S(2)}) %copy-start.3) | copy-done | bytes 1048600
  45.3 2.5 %shard_map.74 = (f32[256,512]{1,0:T(8,128)S(1)}, f32[256,128]{1,0:T(8,128)S(1)}, f32[256,128]{1,0:T(8,128)S(1)}) custom-call(bf16[4096,512]{1,0:T(8,128)(2,1)S(1)} %copy-done, bf16[4096,128]{1,0:T(8,128)(2,1)S(1)} %copy-done.3, bf16[4096,128]{1,0:T(8,128)(2,1)S(1)} %copy-done.5, bf16[256,512]{1,0:T(8,128)(2,1)S(1)} %get-tuple-element.69.refs_0_, ...), custom_call_target="tpu_custom_call" | custom-call | tf_op jit(solution)/shard_map/pallas_call | solution.py:143
  47.9 2.5 %shard_map.78 = (f32[256,512]{1,0:T(8,128)S(1)}, f32[256,128]{1,0:T(8,128)S(1)}, f32[256,128]{1,0:T(8,128)S(1)}) custom-call(bf16[4096,512]{1,0:T(8,128)(2,1)S(1)} %copy-done, bf16[4096,128]{1,0:T(8,128)(2,1)S(1)} %copy-done.3, bf16[4096,128]{1,0:T(8,128)(2,1)S(1)} %copy-done.5, bf16[256,512]{1,0:T(8,128)(2,1)S(1)} %get-tuple-element.70.refs_0_, ...), custom_call_target="tpu_custom_call" | custom-call | tf_op jit(solution)/shard_map/pallas_call | solution.py:143
  50.4 1.4 %shard_map.75 = (bf16[256,512]{1,0:T(8,128)(2,1)S(1)}, bf16[256,128]{1,0:T(8,128)(2,1)S(1)}, bf16[256,128]{1,0:T(8,128)(2,1)S(1)}, bf16[256,512]{1,0:T(8,128)(2,1)S(1)}, bf16[256,512]{1,0:T(8,128)(2,1)S(1)}) custom-call(bf16[256,512]{1,0:T(8,128)(2,1)S(1)} %collective-permute-done.3.far, f32[256,512]{1,0:T(8,128)S(1)} %get-tuple-element.39.q, ...), custom_call_target="tpu_custom_call" | custom-call | tf_op jit(solution)/shard_map/pallas_call | solution.py:143
  51.7 2.1 %shard_map.79 = (bf16[256,512]{1,0:T(8,128)(2,1)S(1)}, bf16[256,512]{1,0:T(8,128)(2,1)S(1)}, bf16[256,512]{1,0:T(8,128)(2,1)S(1)}) custom-call(bf16[256,512]{1,0:T(8,128)(2,1)S(1)} %collective-permute-done.17.far, f32[256,512]{1,0:T(8,128)S(1)} %get-tuple-element.52.q, f32[256,128]{1,0:T(8,128)S(1)} %get-tuple-element.53.k, ...), custom_call_target="tpu_custom_call" | custom-call | tf_op jit(solution)/shard_map/pallas_call | solution.py:143
  53.9 3.5 %collective-permute-start.24 = (bf16[256,512]{1,0:T(8,128)(2,1)S(1)}, bf16[256,512]{1,0:T(8,128)(2,1)S(1)}, u32[]{:S(2)}, u32[]{:S(2)}) collective-permute-start(bf16[256,512]{1,0:T(8,128)(2,1)S(1)} %get-tuple-element.65), channel_id=1, source_target_pairs={{0,7},{1,0},{2,1},{3,2},{4,3},{5,4},{6,5},{7,6},{8,15},{9,8},{10,9... | collective-permute-start | bytes 786440 | tf_op jit(solution)/shard_map/ppermute | solution.py:163
  57.4 2.7 %collective-permute-start.11 = (bf16[256,512]{1,0:T(8,128)(2,1)S(1)}, bf16[256,512]{1,0:T(8,128)(2,1)S(1)}, u32[]{:S(2)}, u32[]{:S(2)}) collective-permute-start(bf16[256,512]{1,0:T(8,128)(2,1)S(1)} %get-tuple-element.50), channel_id=1, source_target_pairs={{0,7},{1,0},{2,1},{3,2},{4,3},{5,4},{6,5},{7,6},{8,15},{9,8},{10,9... | collective-permute-start | bytes 786440 | tf_op jit(solution)/shard_map/ppermute | solution.py:163
  62.6 2.7 %collective-permute-start.25 = (bf16[256,512]{1,0:T(8,128)(2,1)S(1)}, bf16[256,512]{1,0:T(8,128)(2,1)S(1)}, u32[]{:S(2)}, u32[]{:S(2)}) collective-permute-start(bf16[256,512]{1,0:T(8,128)(2,1)S(1)} %add_convert_fusion.2), channel_id=1, source_target_pairs={{0,7},{1,0},{2,1},{3,2},{4,3},{5,4},{6,5},{7,6},{8,15},{9,8},{10,9... | collective-permute-start | bytes 786440 | tf_op jit(solution)/shard_map/ppermute | solution.py:163
  65.3 1.6 %collective-permute-done.7 = bf16[256,512]{1,0:T(8,128)(2,1)S(1)} collective-permute-done((bf16[256,512]{1,0:T(8,128)(2,1)S(1)}, bf16[256,512]{1,0:T(8,128)(2,1)S(1)}, u32[]{:S(2)}, u32[]{:S(2)}) %collective-permute-start.7) | collective-permute-done | bytes 262176 | tf_op jit(solution)/shard_map/ppermute | solution.py:163
  67.2 2.7 %collective-permute-start.12 = (bf16[256,512]{1,0:T(8,128)(2,1)S(1)}, bf16[256,512]{1,0:T(8,128)(2,1)S(1)}, u32[]{:S(2)}, u32[]{:S(2)}) collective-permute-start(bf16[256,512]{1,0:T(8,128)(2,1)S(1)} %add_convert_fusion.6), channel_id=1, source_target_pairs={{0,7},{1,0},{2,1},{3,2},{4,3},{5,4},{6,5},{7,6},{8,15},{9,8},{10,9... | collective-permute-start | bytes 786440 | tf_op jit(solution)/shard_map/ppermute | solution.py:163
  69.9 2.6 %collective-permute-done.22 = bf16[256,512]{1,0:T(8,128)(2,1)S(1)} collective-permute-done((bf16[256,512]{1,0:T(8,128)(2,1)S(1)}, bf16[256,512]{1,0:T(8,128)(2,1)S(1)}, u32[]{:S(2)}, u32[]{:S(2)}) %collective-permute-start.22) | collective-permute-done | bytes 262176 | tf_op jit(solution)/shard_map/ppermute | solution.py:163
  72.7 5.5 %collective-permute-done.8 = bf16[256,512]{1,0:T(8,128)(2,1)S(1)} collective-permute-done((bf16[256,512]{1,0:T(8,128)(2,1)S(1)}, bf16[256,512]{1,0:T(8,128)(2,1)S(1)}, u32[]{:S(2)}, u32[]{:S(2)}) %collective-permute-start.8) | collective-permute-done | bytes 262176 | tf_op jit(solution)/shard_map/ppermute | solution.py:163
  78.4 2.7 %collective-permute-start.26 = (bf16[256,512]{1,0:T(8,128)(2,1)S(1)}, bf16[256,512]{1,0:T(8,128)(2,1)S(1)}, u32[]{:S(2)}, u32[]{:S(2)}) collective-permute-start(bf16[256,512]{1,0:T(8,128)(2,1)S(1)} %add_convert_fusion.1), channel_id=1, source_target_pairs={{0,7},{1,0},{2,1},{3,2},{4,3},{5,4},{6,5},{7,6},{8,15},{9,8},{10,9... | collective-permute-start | bytes 786440 | tf_op jit(solution)/shard_map/ppermute | solution.py:163
  81.3 8.1 %collective-permute-done.9 = bf16[256,512]{1,0:T(8,128)(2,1)S(1)} collective-permute-done((bf16[256,512]{1,0:T(8,128)(2,1)S(1)}, bf16[256,512]{1,0:T(8,128)(2,1)S(1)}, u32[]{:S(2)}, u32[]{:S(2)}) %collective-permute-start.9) | collective-permute-done | bytes 262176 | tf_op jit(solution)/shard_map/ppermute | solution.py:163
  89.7 2.7 %collective-permute-start.27 = (bf16[256,512]{1,0:T(8,128)(2,1)S(1)}, bf16[256,512]{1,0:T(8,128)(2,1)S(1)}, u32[]{:S(2)}, u32[]{:S(2)}) collective-permute-start(bf16[256,512]{1,0:T(8,128)(2,1)S(1)} %add_convert_fusion), channel_id=1, source_target_pairs={{0,7},{1,0},{2,1},{3,2},{4,3},{5,4},{6,5},{7,6},{8,15},{9,8},{10,9... | collective-permute-start | bytes 786440 | tf_op jit(solution)/shard_map/ppermute | solution.py:163
  93.1 1.4 %shard_map.73 = (bf16[512,512]{1,0:T(8,128)(2,1)S(1)}, bf16[512,128]{1,0:T(8,128)(2,1)S(1)}) custom-call(s32[32,32]{1,0:T(8,128)S(1)} %copy-done.7), custom_call_target="tpu_custom_call" | custom-call | tf_op jit(solution)/shard_map/pallas_call | solution.py:143
  94.5 1.4 %collective-permute-done.10.up = bf16[256,512]{1,0:T(8,128)(2,1)S(1)} collective-permute-done((bf16[256,512]{1,0:T(8,128)(2,1)S(1)}, bf16[256,512]{1,0:T(8,128)(2,1)S(1)}, u32[]{:S(2)}, u32[]{:S(2)}) %collective-permute-start.10) | collective-permute-done | bytes 262176 | tf_op jit(solution)/shard_map/ppermute | solution.py:163
  97.3 22.2 %all_to_all.5 = bf16[32,16,512]{2,1,0:T(8,128)(2,1)S(1)} all-to-all(bf16[32,16,512]{2,1,0:T(8,128)(2,1)S(1)} %bitcast.3), channel_id=1, replica_groups=mesh['dp'=32,'tensor'=8] {'dp'}, dimensions={0} | all-to-all | bytes 1048576 | tf_op jit(solution)/shard_map/all_to_all | solution.py:251
  (66 shorter events, 11.2 us)
Async XLA Ops:
  1.1 12.5 %collective-permute-start = (bf16[256,512]{1,0:T(8,128)(2,1)S(1)}, bf16[256,512]{1,0:T(8,128)(2,1)S(1)}, u32[]{:S(2)}, u32[]{:S(2)}) collective-permute-start(bf16[256,512]{1,0:T(8,128)(2,1)S(1)} %get-tuple-element.69.refs_0_), channel_id=1, source_target_pairs={{0,1},{1,2},{2,3},{3,4},{4,5},{5,6},{6,7},{7,0},{8,9},{9,10},{10,1... | collective-permute-start | bytes 786440 | tf_op jit(solution)/shard_map/ppermute | solution.py:163
  3.6 10.0 %collective-permute-start.14 = (bf16[256,512]{1,0:T(8,128)(2,1)S(1)}, bf16[256,512]{1,0:T(8,128)(2,1)S(1)}, u32[]{:S(2)}, u32[]{:S(2)}) collective-permute-start(bf16[256,512]{1,0:T(8,128)(2,1)S(1)} %get-tuple-element.70.refs_0_), channel_id=1, source_target_pairs={{0,7},{1,0},{2,1},{3,2},{4,3},{5,4},{6,5},{7,6},{8,15},{9,8},{10,9... | collective-permute-start | bytes 786440 | tf_op jit(solution)/shard_map/ppermute | solution.py:163
  7.6 10.6 %collective-permute-start.4 = (bf16[256,512]{1,0:T(8,128)(2,1)S(1)}, bf16[256,512]{1,0:T(8,128)(2,1)S(1)}, u32[]{:S(2)}, u32[]{:S(2)}) collective-permute-start(bf16[256,512]{1,0:T(8,128)(2,1)S(1)} %get-tuple-element.69.refs_0_), channel_id=1, source_target_pairs={{0,7},{1,0},{2,1},{3,2},{4,3},{5,4},{6,5},{7,6},{8,15},{9,8},{10,9... | collective-permute-start | bytes 786440 | tf_op jit(solution)/shard_map/ppermute | solution.py:163
  9.0 12.6 %collective-permute-start.18 = (bf16[256,512]{1,0:T(8,128)(2,1)S(1)}, bf16[256,512]{1,0:T(8,128)(2,1)S(1)}, u32[]{:S(2)}, u32[]{:S(2)}) collective-permute-start(bf16[256,512]{1,0:T(8,128)(2,1)S(1)} %get-tuple-element.70.refs_0_), channel_id=1, source_target_pairs={{0,1},{1,2},{2,3},{3,4},{4,5},{5,6},{6,7},{7,0},{8,9},{9,10},{10,1... | collective-permute-start | bytes 786440 | tf_op jit(solution)/shard_map/ppermute | solution.py:163
  13.5 11.2 %collective-permute-start.1 = (bf16[256,512]{1,0:T(8,128)(2,1)S(1)}, bf16[256,512]{1,0:T(8,128)(2,1)S(1)}, u32[]{:S(2)}, u32[]{:S(2)}) collective-permute-start(bf16[256,512]{1,0:T(8,128)(2,1)S(1)} %collective-permute-done.refs_1_), channel_id=1, source_target_pairs={{0,1},{1,2},{2,3},{3,4},{4,5},{5,6},{6,7},{7,0},{8,9},{9,10},{10,1... | collective-permute-start | bytes 786440 | tf_op jit(solution)/shard_map/ppermute | solution.py:163
  13.6 11.2 %collective-permute-start.15 = (bf16[256,512]{1,0:T(8,128)(2,1)S(1)}, bf16[256,512]{1,0:T(8,128)(2,1)S(1)}, u32[]{:S(2)}, u32[]{:S(2)}) collective-permute-start(bf16[256,512]{1,0:T(8,128)(2,1)S(1)} %collective-permute-done.14.refs_2_), channel_id=1, source_target_pairs={{0,7},{1,0},{2,1},{3,2},{4,3},{5,4},{6,5},{7,6},{8,15},{9,8},{10,9... | collective-permute-start | bytes 786440 | tf_op jit(solution)/shard_map/ppermute | solution.py:163
  18.2 11.2 %collective-permute-start.5 = (bf16[256,512]{1,0:T(8,128)(2,1)S(1)}, bf16[256,512]{1,0:T(8,128)(2,1)S(1)}, u32[]{:S(2)}, u32[]{:S(2)}) collective-permute-start(bf16[256,512]{1,0:T(8,128)(2,1)S(1)} %collective-permute-done.4.refs_2_), channel_id=1, source_target_pairs={{0,7},{1,0},{2,1},{3,2},{4,3},{5,4},{6,5},{7,6},{8,15},{9,8},{10,9... | collective-permute-start | bytes 786440 | tf_op jit(solution)/shard_map/ppermute | solution.py:163
  21.7 11.2 %collective-permute-start.19 = (bf16[256,512]{1,0:T(8,128)(2,1)S(1)}, bf16[256,512]{1,0:T(8,128)(2,1)S(1)}, u32[]{:S(2)}, u32[]{:S(2)}) collective-permute-start(bf16[256,512]{1,0:T(8,128)(2,1)S(1)} %collective-permute-done.18.refs_1_), channel_id=1, source_target_pairs={{0,1},{1,2},{2,3},{3,4},{4,5},{5,6},{6,7},{7,0},{8,9},{9,10},{10,1... | collective-permute-start | bytes 786440 | tf_op jit(solution)/shard_map/ppermute | solution.py:163
  24.8 9.3 %collective-permute-start.2 = (bf16[256,512]{1,0:T(8,128)(2,1)S(1)}, bf16[256,512]{1,0:T(8,128)(2,1)S(1)}, u32[]{:S(2)}, u32[]{:S(2)}) collective-permute-start(bf16[256,512]{1,0:T(8,128)(2,1)S(1)} %collective-permute-done.1.refs_3_), channel_id=1, source_target_pairs={{0,1},{1,2},{2,3},{3,4},{4,5},{5,6},{6,7},{7,0},{8,9},{9,10},{10,1... | collective-permute-start | bytes 786440 | tf_op jit(solution)/shard_map/ppermute | solution.py:163
  24.8 10.3 %collective-permute-start.16 = (bf16[256,512]{1,0:T(8,128)(2,1)S(1)}, bf16[256,512]{1,0:T(8,128)(2,1)S(1)}, u32[]{:S(2)}, u32[]{:S(2)}) collective-permute-start(bf16[256,512]{1,0:T(8,128)(2,1)S(1)} %collective-permute-done.15.refs_4_), channel_id=1, source_target_pairs={{0,7},{1,0},{2,1},{3,2},{4,3},{5,4},{6,5},{7,6},{8,15},{9,8},{10,9... | collective-permute-start | bytes 786440 | tf_op jit(solution)/shard_map/ppermute | solution.py:163
  29.5 11.2 %collective-permute-start.6 = (bf16[256,512]{1,0:T(8,128)(2,1)S(1)}, bf16[256,512]{1,0:T(8,128)(2,1)S(1)}, u32[]{:S(2)}, u32[]{:S(2)}) collective-permute-start(bf16[256,512]{1,0:T(8,128)(2,1)S(1)} %collective-permute-done.5.refs_4_), channel_id=1, source_target_pairs={{0,7},{1,0},{2,1},{3,2},{4,3},{5,4},{6,5},{7,6},{8,15},{9,8},{10,9... | collective-permute-start | bytes 786440 | tf_op jit(solution)/shard_map/ppermute | solution.py:163
  32.9 15.0 %collective-permute-start.20 = (bf16[256,512]{1,0:T(8,128)(2,1)S(1)}, bf16[256,512]{1,0:T(8,128)(2,1)S(1)}, u32[]{:S(2)}, u32[]{:S(2)}) collective-permute-start(bf16[256,512]{1,0:T(8,128)(2,1)S(1)} %collective-permute-done.19.refs_3_), channel_id=1, source_target_pairs={{0,1},{1,2},{2,3},{3,4},{4,5},{5,6},{6,7},{7,0},{8,9},{9,10},{10,1... | collective-permute-start | bytes 786440 | tf_op jit(solution)/shard_map/ppermute | solution.py:163
  34.1 16.3 %collective-permute-start.3 = (bf16[256,512]{1,0:T(8,128)(2,1)S(1)}, bf16[256,512]{1,0:T(8,128)(2,1)S(1)}, u32[]{:S(2)}, u32[]{:S(2)}) collective-permute-start(bf16[256,512]{1,0:T(8,128)(2,1)S(1)} %collective-permute-done.2.refs_5_), channel_id=1, source_target_pairs={{0,1},{1,2},{2,3},{3,4},{4,5},{5,6},{6,7},{7,0},{8,9},{9,10},{10,1... | collective-permute-start | bytes 786440 | tf_op jit(solution)/shard_map/ppermute | solution.py:163
  35.1 16.6 %collective-permute-start.17 = (bf16[256,512]{1,0:T(8,128)(2,1)S(1)}, bf16[256,512]{1,0:T(8,128)(2,1)S(1)}, u32[]{:S(2)}, u32[]{:S(2)}) collective-permute-start(bf16[256,512]{1,0:T(8,128)(2,1)S(1)} %collective-permute-done.16.refs_6_), channel_id=1, source_target_pairs={{0,7},{1,0},{2,1},{3,2},{4,3},{5,4},{6,5},{7,6},{8,15},{9,8},{10,9... | collective-permute-start | bytes 786440 | tf_op jit(solution)/shard_map/ppermute | solution.py:163
  47.8 2.5 %copy-start.2 = (bf16[512,4096]{1,0:T(8,128)(2,1)S(1)}, bf16[512,4096]{1,0:T(8,128)(2,1)}, u32[]{:S(2)}) copy-start(bf16[512,4096]{1,0:T(8,128)(2,1)} %refs_0_.2) | copy-start | bytes 12582916
  53.8 8.3 %collective-permute-start.21 = (bf16[256,512]{1,0:T(8,128)(2,1)S(1)}, bf16[256,512]{1,0:T(8,128)(2,1)S(1)}, u32[]{:S(2)}, u32[]{:S(2)}) collective-permute-start(bf16[256,512]{1,0:T(8,128)(2,1)S(1)} %get-tuple-element.61), channel_id=1, source_target_pairs={{0,1},{1,2},{2,3},{3,4},{4,5},{5,6},{6,7},{7,0},{8,9},{9,10},{10,1... | collective-permute-start | bytes 786440 | tf_op jit(solution)/shard_map/ppermute | solution.py:163
  53.9 8.6 %collective-permute-start.24 = (bf16[256,512]{1,0:T(8,128)(2,1)S(1)}, bf16[256,512]{1,0:T(8,128)(2,1)S(1)}, u32[]{:S(2)}, u32[]{:S(2)}) collective-permute-start(bf16[256,512]{1,0:T(8,128)(2,1)S(1)} %get-tuple-element.65), channel_id=1, source_target_pairs={{0,7},{1,0},{2,1},{3,2},{4,3},{5,4},{6,5},{7,6},{8,15},{9,8},{10,9... | collective-permute-start | bytes 786440 | tf_op jit(solution)/shard_map/ppermute | solution.py:163
  57.4 9.6 %collective-permute-start.7 = (bf16[256,512]{1,0:T(8,128)(2,1)S(1)}, bf16[256,512]{1,0:T(8,128)(2,1)S(1)}, u32[]{:S(2)}, u32[]{:S(2)}) collective-permute-start(bf16[256,512]{1,0:T(8,128)(2,1)S(1)} %get-tuple-element.47), channel_id=1, source_target_pairs={{0,1},{1,2},{2,3},{3,4},{4,5},{5,6},{6,7},{7,0},{8,9},{9,10},{10,1... | collective-permute-start | bytes 786440 | tf_op jit(solution)/shard_map/ppermute | solution.py:163
  57.4 9.7 %collective-permute-start.11 = (bf16[256,512]{1,0:T(8,128)(2,1)S(1)}, bf16[256,512]{1,0:T(8,128)(2,1)S(1)}, u32[]{:S(2)}, u32[]{:S(2)}) collective-permute-start(bf16[256,512]{1,0:T(8,128)(2,1)S(1)} %get-tuple-element.50), channel_id=1, source_target_pairs={{0,7},{1,0},{2,1},{3,2},{4,3},{5,4},{6,5},{7,6},{8,15},{9,8},{10,9... | collective-permute-start | bytes 786440 | tf_op jit(solution)/shard_map/ppermute | solution.py:163
  62.2 10.3 %collective-permute-start.22 = (bf16[256,512]{1,0:T(8,128)(2,1)S(1)}, bf16[256,512]{1,0:T(8,128)(2,1)S(1)}, u32[]{:S(2)}, u32[]{:S(2)}) collective-permute-start(bf16[256,512]{1,0:T(8,128)(2,1)S(1)} %add_convert_fusion.4), channel_id=1, source_target_pairs={{0,1},{1,2},{2,3},{3,4},{4,5},{5,6},{6,7},{7,0},{8,9},{9,10},{10,1... | collective-permute-start | bytes 786440 | tf_op jit(solution)/shard_map/ppermute | solution.py:163
  62.6 15.7 %collective-permute-start.25 = (bf16[256,512]{1,0:T(8,128)(2,1)S(1)}, bf16[256,512]{1,0:T(8,128)(2,1)S(1)}, u32[]{:S(2)}, u32[]{:S(2)}) collective-permute-start(bf16[256,512]{1,0:T(8,128)(2,1)S(1)} %add_convert_fusion.2), channel_id=1, source_target_pairs={{0,7},{1,0},{2,1},{3,2},{4,3},{5,4},{6,5},{7,6},{8,15},{9,8},{10,9... | collective-permute-start | bytes 786440 | tf_op jit(solution)/shard_map/ppermute | solution.py:163
  67.0 11.2 %collective-permute-start.8 = (bf16[256,512]{1,0:T(8,128)(2,1)S(1)}, bf16[256,512]{1,0:T(8,128)(2,1)S(1)}, u32[]{:S(2)}, u32[]{:S(2)}) collective-permute-start(bf16[256,512]{1,0:T(8,128)(2,1)S(1)} %add_convert_fusion.9), channel_id=1, source_target_pairs={{0,1},{1,2},{2,3},{3,4},{4,5},{5,6},{6,7},{7,0},{8,9},{9,10},{10,1... | collective-permute-start | bytes 786440 | tf_op jit(solution)/shard_map/ppermute | solution.py:163
  67.2 14.0 %collective-permute-start.12 = (bf16[256,512]{1,0:T(8,128)(2,1)S(1)}, bf16[256,512]{1,0:T(8,128)(2,1)S(1)}, u32[]{:S(2)}, u32[]{:S(2)}) collective-permute-start(bf16[256,512]{1,0:T(8,128)(2,1)S(1)} %add_convert_fusion.6), channel_id=1, source_target_pairs={{0,7},{1,0},{2,1},{3,2},{4,3},{5,4},{6,5},{7,6},{8,15},{9,8},{10,9... | collective-permute-start | bytes 786440 | tf_op jit(solution)/shard_map/ppermute | solution.py:163
  72.5 19.9 %copy-start.1 = (bf16[4096,512]{1,0:T(8,128)(2,1)S(1)}, bf16[4096,512]{1,0:T(8,128)(2,1)}, u32[]{:S(2)}) copy-start(bf16[4096,512]{1,0:T(8,128)(2,1)} %refs_1_.2) | copy-start | bytes 12582916
  72.6 23.8 %collective-permute-start.23 = (bf16[256,512]{1,0:T(8,128)(2,1)S(1)}, bf16[256,512]{1,0:T(8,128)(2,1)S(1)}, u32[]{:S(2)}, u32[]{:S(2)}) collective-permute-start(bf16[256,512]{1,0:T(8,128)(2,1)S(1)} %add_convert_fusion.3), channel_id=1, source_target_pairs={{0,1},{1,2},{2,3},{3,4},{4,5},{5,6},{6,7},{7,0},{8,9},{9,10},{10,1... | collective-permute-start | bytes 786440 | tf_op jit(solution)/shard_map/ppermute | solution.py:163
  78.2 11.2 %collective-permute-start.9 = (bf16[256,512]{1,0:T(8,128)(2,1)S(1)}, bf16[256,512]{1,0:T(8,128)(2,1)S(1)}, u32[]{:S(2)}, u32[]{:S(2)}) collective-permute-start(bf16[256,512]{1,0:T(8,128)(2,1)S(1)} %add_convert_fusion.8), channel_id=1, source_target_pairs={{0,1},{1,2},{2,3},{3,4},{4,5},{5,6},{6,7},{7,0},{8,9},{9,10},{10,1... | collective-permute-start | bytes 786440 | tf_op jit(solution)/shard_map/ppermute | solution.py:163
  78.4 11.2 %collective-permute-start.26 = (bf16[256,512]{1,0:T(8,128)(2,1)S(1)}, bf16[256,512]{1,0:T(8,128)(2,1)S(1)}, u32[]{:S(2)}, u32[]{:S(2)}) collective-permute-start(bf16[256,512]{1,0:T(8,128)(2,1)S(1)} %add_convert_fusion.1), channel_id=1, source_target_pairs={{0,7},{1,0},{2,1},{3,2},{4,3},{5,4},{6,5},{7,6},{8,15},{9,8},{10,9... | collective-permute-start | bytes 786440 | tf_op jit(solution)/shard_map/ppermute | solution.py:163
  81.2 13.3 %collective-permute-start.13 = (bf16[256,512]{1,0:T(8,128)(2,1)S(1)}, bf16[256,512]{1,0:T(8,128)(2,1)S(1)}, u32[]{:S(2)}, u32[]{:S(2)}) collective-permute-start(bf16[256,512]{1,0:T(8,128)(2,1)S(1)} %add_convert_fusion.5), channel_id=1, source_target_pairs={{0,7},{1,0},{2,1},{3,2},{4,3},{5,4},{6,5},{7,6},{8,15},{9,8},{10,9... | collective-permute-start | bytes 786440 | tf_op jit(solution)/shard_map/ppermute | solution.py:163
  89.5 6.5 %collective-permute-start.10 = (bf16[256,512]{1,0:T(8,128)(2,1)S(1)}, bf16[256,512]{1,0:T(8,128)(2,1)S(1)}, u32[]{:S(2)}, u32[]{:S(2)}) collective-permute-start(bf16[256,512]{1,0:T(8,128)(2,1)S(1)} %add_convert_fusion.7), channel_id=1, source_target_pairs={{0,1},{1,2},{2,3},{3,4},{4,5},{5,6},{6,7},{7,0},{8,9},{9,10},{10,1... | collective-permute-start | bytes 786440 | tf_op jit(solution)/shard_map/ppermute | solution.py:163
  89.6 2.8 %copy-start.4 = (bf16[4096,128]{1,0:T(8,128)(2,1)S(1)}, bf16[4096,128]{1,0:T(8,128)(2,1)}, u32[]{:S(2)}) copy-start(bf16[4096,128]{1,0:T(8,128)(2,1)} %refs_0_.3) | copy-start | bytes 3145732
  89.6 2.8 %copy-start.6 = (bf16[4096,128]{1,0:T(8,128)(2,1)S(1)}, bf16[4096,128]{1,0:T(8,128)(2,1)}, u32[]{:S(2)}) copy-start(bf16[4096,128]{1,0:T(8,128)(2,1)} %refs_1_.3) | copy-start | bytes 3145732
  89.7 7.2 %collective-permute-start.27 = (bf16[256,512]{1,0:T(8,128)(2,1)S(1)}, bf16[256,512]{1,0:T(8,128)(2,1)S(1)}, u32[]{:S(2)}, u32[]{:S(2)}) collective-permute-start(bf16[256,512]{1,0:T(8,128)(2,1)S(1)} %add_convert_fusion), channel_id=1, source_target_pairs={{0,7},{1,0},{2,1},{3,2},{4,3},{5,4},{6,5},{7,6},{8,15},{9,8},{10,9... | collective-permute-start | bytes 786440 | tf_op jit(solution)/shard_map/ppermute | solution.py:163
  (5 other events, 7.9 us)
